TPU v7x, 512 devices: a whole 4x8x8 slice. The times are simulated.
512 devices in a mesh: batch: 128 (over x, z, y_hi), mp: 4 (over y_lo, core).
Axes of the slice: x: 4, y: 8 (y_hi: 4, y_lo: 2; y = y_hi * 2 + y_lo), z: 8, core: 2. Of those that a mesh axis runs over, the one named last changes fastest.
Arguments:
- query_hidden: bfloat16 [131072, 768], P(('batch', 'mp')), may hold values from -28 to 28
- passage_hidden: bfloat16 [655360, 768], P(('batch', 'mp')), may hold values from -28 to 28
- projection: bfloat16 [768, 128], replicated, may hold values from -0.21875 to 0.21875
- query_lengths: int32 [4096], P(('batch', 'mp')), may hold values from 8 to 32, as said below
- passage_lengths: int32 [5120], P(('batch', 'mp')), may hold values from 64 to 128, as said below
- positives: int32 [4096], P(('batch', 'mp')), may hold values from 0 to 9
Outputs:
- query_loss: float32 [4096], P(('batch', 'mp'))
- grad_query_hidden: bfloat16 [131072, 768], P(('batch', 'mp'))
- grad_passage_hidden: bfloat16 [655360, 768], P(('batch', 'mp'))
- grad_projection: float32 [768, 128], replicated
Inputs may be any that keep to these rules, and one draw needn't show every extreme that they name: `query_lengths`: the first query of each block of 8 queries has all 32 tokens. `passage_lengths`: the first passage of each block of 10 passages has all 128 tokens.
All inputs are finite; a program needn't handle non-finite values.
Results may differ from a plain program's by a relative error of at most 0.012.
The roundings to bfloat16 on the way count: a program that leaves them out, or rounds other values in their place, can miss the bound.
Values may be sent and summed in bfloat16 or wider, within the bound.
A program may use at most 64 MiB of HBM per device.

v0:
```python
import jax
import jax.numpy as jnp
from jax import lax
from jax.sharding import PartitionSpec as P

inner_scale = 128.0
outer_scale = 8.0
loss_scale = 32.0
norm_eps = 1e-06


def shifted(block, axis, distance):
    devices = range(lax.axis_size(axis))
    route = [((i - distance) % len(devices), i) for i in devices]
    return lax.ppermute(block, axis, route)


def embed_rows(hidden, projection):
    before = jnp.dot(hidden, projection, preferred_element_type=jnp.float32)
    radius = jnp.sqrt(jnp.sum(before * before, axis=-1, keepdims=True) + norm_eps)
    return (before / radius, radius)


def candidate_block(query_embed, passage_embed, passage_valid, query_keep):
    queries, query_tokens = query_keep.shape
    passages, passage_tokens = passage_valid.shape
    sims = jnp.dot(query_embed, passage_embed.T, preferred_element_type=jnp.float32)
    sims = sims.reshape(queries, query_tokens, passages, passage_tokens)
    logits = jnp.where(passage_valid[None, None], sims * inner_scale, -jnp.inf)
    row_top = jnp.max(logits, axis=-1, keepdims=True)
    powers = jnp.exp(logits - row_top)
    totals = jnp.sum(powers, axis=-1, keepdims=True)
    weights = powers / totals
    best = (jnp.log(totals[..., 0]) + row_top[..., 0]) / inner_scale
    scores = outer_scale * jnp.sum(query_keep[:, :, None] * best, axis=1)
    return (scores, weights)


def softmax_loss(scores, positives):
    row_top = jnp.max(scores, axis=1, keepdims=True)
    totals = jnp.sum(jnp.exp(scores - row_top), axis=1, keepdims=True)
    log_total = row_top + jnp.log(totals)
    probs = jnp.exp(scores - log_total)
    columns = jnp.arange(scores.shape[1], dtype=jnp.int32)
    onehot = (columns[None, :] == positives[:, None]).astype(jnp.float32)
    losses = log_total[:, 0] - jnp.sum(onehot * scores, axis=1)
    return (losses, loss_scale * (probs - onehot))


def block_grads(dscores, query_keep, weights, query_embed, passage_embed):
    grad_sim = (
        outer_scale * dscores[:, None, :, None] * query_keep[:, :, None, None] * weights
    ).astype(jnp.bfloat16)
    flat = grad_sim.reshape(query_embed.shape[0], passage_embed.shape[0])
    to_query = jnp.dot(flat, passage_embed, preferred_element_type=jnp.float32)
    to_passage = lax.dot_general(
        flat, query_embed, (((0,), (0,)), ((), ())), preferred_element_type=jnp.float32
    )
    return (to_query, to_passage)


def back_norm(grad, unit, radius):
    return ((grad - unit * jnp.sum(unit * grad, axis=-1, keepdims=True)) / radius).astype(
        jnp.bfloat16
    )


def contract_rows(left, right):
    return lax.dot_general(
        left, right, (((0,), (0,)), ((), ())), preferred_element_type=jnp.float32
    )


def per_device(query_hidden, passage_hidden, projection, query_lengths, passage_lengths, positives):
    queries = query_lengths.shape[0]
    passages = passage_lengths.shape[0]
    query_tokens = query_hidden.shape[0] // queries
    passage_tokens = passage_hidden.shape[0] // passages
    query_unit, query_radius = embed_rows(query_hidden, projection)
    passage_unit, passage_radius = embed_rows(passage_hidden, projection)
    query_embed = query_unit.astype(jnp.bfloat16)
    passage_embed = passage_unit.astype(jnp.bfloat16)
    length_values = passage_lengths.astype(jnp.bfloat16)
    query_keep = (
        jnp.arange(query_tokens, dtype=jnp.int32)[None, :] < query_lengths[:, None]
    ).astype(jnp.float32)
    slots = jnp.arange(passage_tokens, dtype=jnp.float32)
    members = [(passage_embed, length_values)]
    current = (passage_embed, length_values)
    for repeat in range(2):
        current = shifted((current[0], current[1]), "batch", -1)
        members.append(current)
    score_list = []
    weight_list = []
    for member in members:
        valid = slots[None, :] < member[1].astype(jnp.float32)[:, None]
        scores, weights = candidate_block(query_embed, member[0], valid, query_keep)
        score_list.append(scores)
        weight_list.append(weights)
    losses, dscores = softmax_loss(jnp.concatenate(score_list, axis=1), positives)
    query_grad = jnp.zeros(query_unit.shape, jnp.float32)
    passage_terms = []
    for column in range(3):
        to_query, to_passage = block_grads(
            dscores[:, column * passages : (column + 1) * passages],
            query_keep,
            weight_list[column],
            query_embed,
            members[column][0],
        )
        query_grad = query_grad + to_query
        passage_terms.append(to_passage)
    query_pre_grad = back_norm(query_grad, query_unit, query_radius)
    query_partial = contract_rows(query_hidden, query_pre_grad)
    carried = passage_terms[2]
    for repeat in range(2):
        carried = (
            shifted(carried.astype(jnp.bfloat16), "batch", 1).astype(carried.dtype)
            + passage_terms[1 - repeat]
        )
    passage_pre_grad = back_norm(carried, passage_unit, passage_radius)
    grad_query_hidden = jnp.dot(
        query_pre_grad, projection.T, preferred_element_type=jnp.float32
    ).astype(jnp.bfloat16)
    grad_passage_hidden = jnp.dot(
        passage_pre_grad, projection.T, preferred_element_type=jnp.float32
    ).astype(jnp.bfloat16)
    passage_partial = contract_rows(passage_hidden, passage_pre_grad)
    weight_total = lax.psum(query_partial + passage_partial, ("batch", "mp"))
    grad_projection = weight_total / (lax.axis_size("batch") * lax.axis_size("mp"))
    return (losses, grad_query_hidden, grad_passage_hidden, grad_projection)


def solution(mesh):
    in_specs = (
        P(("batch", "mp"), None),
        P(("batch", "mp"), None),
        P(),
        P(("batch", "mp")),
        P(("batch", "mp")),
        P(("batch", "mp")),
    )
    out_specs = (P(("batch", "mp")), P(("batch", "mp"), None), P(("batch", "mp"), None), P())
    return jax.shard_map(
        per_device, mesh=mesh, in_specs=in_specs, out_specs=out_specs, check_vma=False
    )
```

profile of v0, /device:TPU:1, one launch (start us, length us, event | category | flops | bytes accessed | tf_op | source)
XLA Modules:
  0.0 411.5 jit_solution(9129074453687419694)
XLA Ops:
  7.3 1.5 copy-done
  8.7 1.7 multiply_reduce_fusion.1
  11.4 17.4 %collective-permute-start.1 = (bf16[1280,128]{0,1:T(8,128)(2,1)}, bf16[1280,128]{0,1:T(8,128)(2,1)}, u32[]{:S(2)}, u32[]{:S(2)}) collective-permute-start(bf16[1280,128]{0,1:T(8,128)(2,1)} %fusion.16), channel_id=1, source_target_pairs={{4,0},{8,4},{12,8},{16,12},{20,16},{24,20},{28,24},{32,28},{36,32}... | collective-permute-start | bytes 983048 | tf_op jit(solution)/shard_map/ppermute | solution.py:15
  29.3 3.8 collective-permute-start
  36.1 1.3 convolution_multiply_fusion.2
  37.5 1.6 mul.189
  39.0 2.4 select_reduce_fusion.2
  41.4 2.0 exponential_reduce_fusion.2
  45.4 9.0 %collective-permute-start.2 = (bf16[10]{0:T(256)(128)(2,1)}, bf16[10]{0:T(256)(128)(2,1)S(1)}, u32[]{:S(2)}, u32[]{:S(2)}) collective-permute-start(bf16[10]{0:T(256)(128)(2,1)} %collective-permute-done), channel_id=1, source_target_pairs={{4,0},{8,4},{12,8},{16,12},{20,16},{24,20},{28,24},{32,28},{36,32}... | collective-permute-start | bytes 68 | tf_op jit(solution)/shard_map/ppermute | solution.py:15
  55.9 2.4 convolution_multiply_fusion.1
  58.3 2.7 mul.196
  60.9 10.2 %collective-permute-start.3 = (bf16[1280,128]{0,1:T(8,128)(2,1)}, bf16[1280,128]{0,1:T(8,128)(2,1)S(1)}, u32[]{:S(2)}, u32[]{:S(2)}) collective-permute-start(bf16[1280,128]{0,1:T(8,128)(2,1)} %collective-permute-done.1), channel_id=1, source_target_pairs={{4,0},{8,4},{12,8},{16,12},{20,16},{24,20},{28,24},{32,28},{36,32}... | collective-permute-start | bytes 983048 | tf_op jit(solution)/shard_map/ppermute | solution.py:15
  71.2 2.2 select_reduce_fusion.1
  73.4 1.9 exponential_reduce_fusion.1
  75.4 1.1 collective-permute-done.3
  77.2 1.4 convolution_multiply_fusion
  78.7 2.7 mul.200
  81.3 2.4 select_reduce_fusion
  83.7 1.3 exponential_reduce_fusion
  88.4 2.0 fusion.7
  90.4 1.3 fusion.18
  93.7 2.0 fusion.1
  95.9 3.1 collective-permute-start.4
  100.9 2.0 fusion.4
  102.9 1.3 convolution_add_fusion.2
  104.8 5.4 %collective-permute-done.4 = bf16[1280,128]{0,1:T(8,128)(2,1)S(1)} collective-permute-done((bf16[1280,128]{0,1:T(8,128)(2,1)S(1)}, bf16[1280,128]{0,1:T(8,128)(2,1)S(1)}, u32[]{:S(2)}, u32[]{:S(2)}) %collective-permute-start.4) | collective-permute-done | bytes 327712 | tf_op jit(solution)/shard_map/ppermute | solution.py:15
  110.4 1.9 collective-permute-start.5
  112.3 1.0 convolution_convert_fusion.2
  113.6 13.6 %collective-permute-done.5 = bf16[1280,128]{0,1:T(8,128)(2,1)S(1)} collective-permute-done((bf16[1280,128]{0,1:T(8,128)(2,1)S(1)}, bf16[1280,128]{0,1:T(8,128)(2,1)S(1)}, u32[]{:S(2)}, u32[]{:S(2)}) %collective-permute-start.5) | collective-permute-done | bytes 327712 | tf_op jit(solution)/shard_map/ppermute | solution.py:15
  127.6 1.2 fusion.9
  128.8 2.0 convolution_convert_fusion
  130.8 271.9 %all-reduce.2.cloned.1.call-done = f32[768,128]{0,1:T(8,128)} async-done(((f32[768,128]{0,1:T(8,128)}), f32[768,128]{0,1:T(8,128)}) %all-reduce.2.cloned.1.call-update) | async-done | bytes 393232 | tf_op jit(solution)/shard_map/psum | solution.py:129
  (114 shorter events, 19.2 us)
Async XLA Ops:
  7.2 1.6 copy-start
  7.2 27.9 %copy-start.8 = (bf16[768,128]{1,0:T(8,128)(2,1)S(1)}, bf16[768,128]{1,0:T(8,128)(2,1)}, u32[]{:S(2)}) copy-start(bf16[768,128]{1,0:T(8,128)(2,1)} %param.8) | copy-start | bytes 589828
  7.2 21.6 %copy-start.31 = (s32[10]{0:T(128)S(1)}, s32[10]{0:T(128)}, u32[]{:S(2)}) copy-start(s32[10]{0:T(128)} %param.10) | copy-start | bytes 124
  7.2 25.8 %copy-start.29 = (s32[8]{0:T(128)S(1)}, s32[8]{0:T(128)}, u32[]{:S(2)}) copy-start(s32[8]{0:T(128)} %param.9) | copy-start | bytes 100
  7.2 27.9 %copy-start.13 = (bf16[256,768]{1,0:T(8,128)(2,1)S(1)}, bf16[256,768]{1,0:T(8,128)(2,1)}, u32[]{:S(2)}) copy-start(bf16[256,768]{1,0:T(8,128)(2,1)} %param.6) | copy-start | bytes 1179652
  7.2 395.5 %all-reduce.2.cloned.1.call-start = ((), (), s32[]{:S(2)}) async-start(), calls=%async_computation | async-start | bytes 786432 | tf_op jit(solution)/shard_map/psum | solution.py:129
  10.5 25.0 %copy-start.6 = (f32[1280,128]{0,1:T(8,128)}, f32[1280,128]{0,1:T(8,128)S(1)}, u32[]{:S(2)}) copy-start(f32[1280,128]{0,1:T(8,128)S(1)} %get-tuple-element.37) | copy-start | bytes 1966084
  11.4 44.5 %collective-permute-start.1 = (bf16[1280,128]{0,1:T(8,128)(2,1)}, bf16[1280,128]{0,1:T(8,128)(2,1)}, u32[]{:S(2)}, u32[]{:S(2)}) collective-permute-start(bf16[1280,128]{0,1:T(8,128)(2,1)} %fusion.16), channel_id=1, source_target_pairs={{4,0},{8,4},{12,8},{16,12},{20,16},{24,20},{28,24},{32,28},{36,32}... | collective-permute-start | bytes 983048 | tf_op jit(solution)/shard_map/ppermute | solution.py:15
  29.3 14.7 %collective-permute-start = (bf16[10]{0:T(256)(128)(2,1)}, bf16[10]{0:T(256)(128)(2,1)}, u32[]{:S(2)}, u32[]{:S(2)}) collective-permute-start(bf16[10]{0:T(256)(128)(2,1)} %get-tuple-element.33), channel_id=1, source_target_pairs={{4,0},{8,4},{12,8},{16,12},{20,16},{24,20},{28,24},{32,28},{36,32}... | collective-permute-start | bytes 68 | tf_op jit(solution)/shard_map/ppermute | solution.py:15
  39.0 2.4 copy-start.2
  39.0 2.4 copy-start.21
  41.4 2.0 copy-start.9
  45.4 9.8 %collective-permute-start.2 = (bf16[10]{0:T(256)(128)(2,1)}, bf16[10]{0:T(256)(128)(2,1)S(1)}, u32[]{:S(2)}, u32[]{:S(2)}) collective-permute-start(bf16[10]{0:T(256)(128)(2,1)} %collective-permute-done), channel_id=1, source_target_pairs={{4,0},{8,4},{12,8},{16,12},{20,16},{24,20},{28,24},{32,28},{36,32}... | collective-permute-start | bytes 68 | tf_op jit(solution)/shard_map/ppermute | solution.py:15
  60.9 12.5 %copy-start.1 = (f32[8,32,10,128]{3,2,1,0:T(8,128)S(1)}, f32[8,32,10,128]{3,2,1,0:T(8,128)}, u32[]{:S(2)}) copy-start(f32[8,32,10,128]{3,2,1,0:T(8,128)} %mul.196) | copy-start | bytes 3932164
  60.9 15.6 %collective-permute-start.3 = (bf16[1280,128]{0,1:T(8,128)(2,1)}, bf16[1280,128]{0,1:T(8,128)(2,1)S(1)}, u32[]{:S(2)}, u32[]{:S(2)}) collective-permute-start(bf16[1280,128]{0,1:T(8,128)(2,1)} %collective-permute-done.1), channel_id=1, source_target_pairs={{4,0},{8,4},{12,8},{16,12},{20,16},{24,20},{28,24},{32,28},{36,32}... | collective-permute-start | bytes 983048 | tf_op jit(solution)/shard_map/ppermute | solution.py:15
  73.4 2.0 copy-start.11
  81.3 2.4 copy-start.3
  81.3 3.7 copy-start.10
  81.3 3.8 copy-start.12
  81.3 3.8 copy-start.17
  81.3 3.8 copy-start.18
  81.3 3.8 copy-start.23
  83.7 1.8 copy-start.30
  83.7 2.7 copy-start.22
  95.9 14.2 %collective-permute-start.4 = (bf16[1280,128]{0,1:T(8,128)(2,1)S(1)}, bf16[1280,128]{0,1:T(8,128)(2,1)S(1)}, u32[]{:S(2)}, u32[]{:S(2)}) collective-permute-start(bf16[1280,128]{0,1:T(8,128)(2,1)S(1)} %convolution_convert_fusion.1), channel_id=1, source_target_pairs={{508,0},{0,4},{4,8},{8,12},{12,16},{16,20},{20,24},{24,28},{28,32}... | collective-permute-start | bytes 983048 | tf_op jit(solution)/shard_map/ppermute | solution.py:15
  99.6 1.3 copy-start.4
  100.9 3.4 copy-start.16
  100.9 3.4 copy-start.20
  100.9 3.4 copy-start.25
  104.3 9.1 %copy-start.14 = (bf16[256,768]{1,0:T(8,128)(2,1)S(1)}, bf16[256,768]{1,0:T(8,128)(2,1)}, u32[]{:S(2)}) copy-start(bf16[256,768]{1,0:T(8,128)(2,1)} %param.6) | copy-start | bytes 1179652
  104.3 22.9 %copy-start.7 = (f32[1280,128]{0,1:T(8,128)S(1)}, f32[1280,128]{0,1:T(8,128)}, u32[]{:S(2)}) copy-start(f32[1280,128]{0,1:T(8,128)} %copy-done.6) | copy-start | bytes 1966084
  110.4 16.8 %collective-permute-start.5 = (bf16[1280,128]{0,1:T(8,128)(2,1)S(1)}, bf16[1280,128]{0,1:T(8,128)(2,1)S(1)}, u32[]{:S(2)}, u32[]{:S(2)}) collective-permute-start(bf16[1280,128]{0,1:T(8,128)(2,1)S(1)} %add_convert_fusion), channel_id=1, source_target_pairs={{508,0},{0,4},{4,8},{8,12},{12,16},{16,20},{20,24},{24,28},{28,32}... | collective-permute-start | bytes 983048 | tf_op jit(solution)/shard_map/ppermute | solution.py:15
  (7 other events, 7.2 us)
Sparse Core Ops, SparseCore 0:
  129.0 273.7 all-reduce.1
where the time goes:
time: 412 us
  waiting for transfers between devices  293 us (71%)
  starting transfers between devices  45.4 us (11%)
  other arithmetic  26.7 us (6%)
  local copies, waits for them, and re-layouts  16.6 us (4%)
  matrix products  15.4 us (4%)
  between operations  14.7 us (4%)
    psum x1, waiting for transfers between devices, per_device(): weight_total = lax.psum(query_partial + passage_partial, ('batch', 'mp'))  272 us
    ppermute x6, starting transfers between devices, shifted(): return lax.ppermute(block, axis, route)  45.3 us
    ppermute x6, waiting for transfers between devices, shifted(): return lax.ppermute(block, axis, route)  20.9 us
  transfers between devices with their start and end apart: 7, of which 5 were waited for; matrix products, arithmetic and copies ran while one was open for 6% of the time, Pallas kernels for 0%

commit v1 on v0

v1 whole, which is shorter than its diff:
```python
import functools

import jax
import jax.numpy as jnp
from jax import lax
from jax.experimental import pallas as pl
from jax.experimental.pallas import tpu as pltpu
from jax.sharding import PartitionSpec as P

inner_scale = 128.0
outer_scale = 8.0
loss_scale = 32.0
norm_eps = 1e-06

NX, NZ, NYH, NMP = 4, 8, 4, 4
NG = NYH * NMP
MESH = pl.DeviceIdType.MESH


def shifted(block, distance):
    count = NX * NZ * NYH
    return lax.ppermute(block, "batch", [(i, (i + distance) % count) for i in range(count)])


def reduce_kernel(src, out, r1, b2, b3, g4, s1, q1, s2, q2, s3, q3, s4, q4):
    bi = lax.axis_index("batch")
    mi = lax.axis_index("mp")
    yh = bi % NYH
    z = (bi // NYH) % NZ
    x = bi // (NYH * NZ)
    g = yh * NMP + mi
    rows = src.shape[0] // NG

    def group_peer(o):
        j = (g + o) % NG
        return j, (bi - yh + j // NMP, j % NMP)

    def z_peer(o):
        j = (z + o) % NZ
        return j, (x * (NZ * NYH) + j * NYH + yh, mi)

    def x_peer(o):
        j = (x + o) % NX
        return j, (j * (NZ * NYH) + z * NYH + yh, mi)

    barrier = pltpu.get_barrier_semaphore()
    for count, peer in ((NG, group_peer), (NZ, z_peer), (NX, x_peer)):
        @pl.loop(1, count)
        def _(o):
            pl.semaphore_signal(barrier, inc=1, device_id=peer(o)[1], device_id_type=MESH)
    pl.semaphore_wait(barrier, NG + NZ + NX - 3)

    def piece(j):
        return pl.ds(pl.multiple_of(j * rows, rows), rows)

    def exchange(count, peer, source, target, mine, send, recv):
        def copy(o):
            j, where = peer(o)
            return pltpu.make_async_remote_copy(
                src_ref=source(j), dst_ref=target(mine), send_sem=send.at[o], recv_sem=recv.at[mine],
                device_id=where, device_id_type=MESH)

        def arrival(o):
            j, where = peer(o)
            return pltpu.make_async_remote_copy(
                src_ref=source(j), dst_ref=target(j), send_sem=send.at[o], recv_sem=recv.at[j],
                device_id=where, device_id_type=MESH)

        @pl.loop(1, count)
        def _(o):
            copy(o).start()

        @pl.loop(1, count)
        def _(o):
            arrival(o).wait_recv()

        @pl.loop(1, count)
        def _(o):
            copy(o).wait_send()

    r1[g] = src[piece(g), :]
    exchange(NG, group_peer, lambda j: src.at[piece(j)], lambda j: r1.at[j], g, s1, q1)
    b2[z] = jnp.sum(r1[...].astype(jnp.float32), axis=0).astype(jnp.bfloat16)
    exchange(NZ, z_peer, lambda j: b2.at[z], lambda j: b2.at[j], z, s2, q2)
    b3[x] = jnp.sum(b2[...].astype(jnp.float32), axis=0).astype(jnp.bfloat16)
    exchange(NX, x_peer, lambda j: b3.at[x], lambda j: b3.at[j], x, s3, q3)
    g4[piece(g), :] = jnp.sum(b3[...].astype(jnp.float32), axis=0).astype(jnp.bfloat16)
    exchange(NG, group_peer, lambda j: g4.at[piece(g)], lambda j: g4.at[piece(j)], g, s4, q4)
    out[...] = g4[...].astype(jnp.float32) * (1.0 / (NX * NZ * NYH * NMP))


def reduce_all(partial):
    rows, dim = partial.shape
    part = rows // NG
    dma = pltpu.SemaphoreType.DMA
    return pl.pallas_call(
        reduce_kernel,
        out_shape=jax.ShapeDtypeStruct((rows, dim), jnp.float32),
        in_specs=[pl.BlockSpec(memory_space=pltpu.VMEM)],
        out_specs=pl.BlockSpec(memory_space=pltpu.VMEM),
        scratch_shapes=[
            pltpu.VMEM((NG, part, dim), jnp.bfloat16),
            pltpu.VMEM((NZ, part, dim), jnp.bfloat16),
            pltpu.VMEM((NX, part, dim), jnp.bfloat16),
            pltpu.VMEM((rows, dim), jnp.bfloat16),
            dma((NG,)), dma((NG,)), dma((NZ,)), dma((NZ,)), dma((NX,)), dma((NX,)), dma((NG,)), dma((NG,)),
        ],
        compiler_params=pltpu.CompilerParams(collective_id=0, has_side_effects=True),
    )(partial)


def embed_rows(hidden, projection):
    before = jnp.dot(hidden, projection, preferred_element_type=jnp.float32)
    radius = jnp.sqrt(jnp.sum(before * before, axis=-1, keepdims=True) + norm_eps)
    return (before / radius, radius)


def candidate_block(query_embed, passage_embed, passage_valid, query_keep):
    queries, query_tokens = query_keep.shape
    passages, passage_tokens = passage_valid.shape
    sims = jnp.dot(query_embed, passage_embed.T, preferred_element_type=jnp.float32)
    sims = sims.reshape(queries, query_tokens, passages, passage_tokens)
    logits = jnp.where(passage_valid[None, None], sims * inner_scale, -jnp.inf)
    row_top = jnp.max(logits, axis=-1, keepdims=True)
    powers = jnp.exp(logits - row_top)
    totals = jnp.sum(powers, axis=-1, keepdims=True)
    weights = powers / totals
    best = (jnp.log(totals[..., 0]) + row_top[..., 0]) / inner_scale
    scores = outer_scale * jnp.sum(query_keep[:, :, None] * best, axis=1)
    return (scores, weights)


def back_norm(grad, unit, radius):
    return ((grad - unit * jnp.sum(unit * grad, axis=-1, keepdims=True)) / radius).astype(
        jnp.bfloat16
    )


def contract_rows(left, right):
    return lax.dot_general(
        left, right, (((0,), (0,)), ((), ())), preferred_element_type=jnp.float32
    )


def per_device(query_hidden, passage_hidden, projection, query_lengths, passage_lengths, positives):
    queries = query_lengths.shape[0]
    passages = passage_lengths.shape[0]
    query_tokens = query_hidden.shape[0] // queries
    passage_tokens = passage_hidden.shape[0] // passages
    query_unit, query_radius = embed_rows(query_hidden, projection)
    query_embed = query_unit.astype(jnp.bfloat16)
    dim = query_embed.shape[1]
    packed = jnp.concatenate(
        [query_embed, jnp.broadcast_to(query_lengths.astype(jnp.bfloat16)[:, None], (queries, dim))], axis=0)
    members = [packed, shifted(packed, 1), shifted(packed, 2)]
    passage_unit, passage_radius = embed_rows(passage_hidden, projection)
    passage_embed = passage_unit.astype(jnp.bfloat16)
    slots = jnp.arange(passage_tokens, dtype=jnp.int32)
    valid = slots[None, :] < passage_lengths[:, None]
    token = jnp.arange(query_tokens, dtype=jnp.float32)
    keeps, embeds, score_list, weight_list = [], [], [], []
    for member in members:
        embed = member[:queries * query_tokens]
        keep = (token[None, :] < member[queries * query_tokens:, :1].astype(jnp.float32)).astype(jnp.float32)
        scores, weights = candidate_block(embed, passage_embed, valid, keep)
        keeps.append(keep)
        embeds.append(embed)
        score_list.append(scores)
        weight_list.append(weights)
    scores = jnp.concatenate(
        [score_list[0], shifted(score_list[1], -1), shifted(score_list[2], -2)], axis=1)
    row_top = jnp.max(scores, axis=1, keepdims=True)
    log_total = row_top + jnp.log(jnp.sum(jnp.exp(scores - row_top), axis=1, keepdims=True))
    columns = jnp.arange(passages, dtype=jnp.int32)
    onehot = (columns[None, :] == positives[:, None]).astype(jnp.float32)
    losses = log_total[:, 0] - jnp.sum(onehot * scores[:, :passages], axis=1)
    log_totals = [log_total, shifted(log_total, 1), shifted(log_total, 2)]
    flats = []
    for b in range(3):
        dscores = jnp.exp(score_list[b] - log_totals[b])
        if b == 0:
            dscores = dscores - onehot
        dscores = loss_scale * dscores
        grad_sim = (
            outer_scale * dscores[:, None, :, None] * keeps[b][:, :, None, None] * weight_list[b]
        ).astype(jnp.bfloat16)
        flats.append(grad_sim.reshape(queries * query_tokens, passages * passage_tokens))
    to_query = [jnp.dot(flat, passage_embed, preferred_element_type=jnp.float32) for flat in flats]
    back1 = shifted(to_query[1].astype(jnp.bfloat16), -1)
    back2 = shifted(to_query[2].astype(jnp.bfloat16), -2)
    passage_grad = sum(contract_rows(flat, embed) for flat, embed in zip(flats, embeds))
    passage_pre_grad = back_norm(passage_grad, passage_unit, passage_radius)
    grad_passage_hidden = jnp.dot(
        passage_pre_grad, projection.T, preferred_element_type=jnp.float32
    ).astype(jnp.bfloat16)
    passage_partial = contract_rows(passage_hidden, passage_pre_grad)
    query_grad = to_query[0] + back1.astype(jnp.float32) + back2.astype(jnp.float32)
    query_pre_grad = back_norm(query_grad, query_unit, query_radius)
    query_partial = contract_rows(query_hidden, query_pre_grad)
    grad_query_hidden = jnp.dot(
        query_pre_grad, projection.T, preferred_element_type=jnp.float32
    ).astype(jnp.bfloat16)
    grad_projection = reduce_all((query_partial + passage_partial).astype(jnp.bfloat16))
    return (losses, grad_query_hidden, grad_passage_hidden, grad_projection)


def solution(mesh):
    in_specs = (
        P(("batch", "mp"), None),
        P(("batch", "mp"), None),
        P(),
        P(("batch", "mp")),
        P(("batch", "mp")),
        P(("batch", "mp")),
    )
    out_specs = (P(("batch", "mp")), P(("batch", "mp"), None), P(("batch", "mp"), None), P())
    return jax.shard_map(
        per_device, mesh=mesh, in_specs=in_specs, out_specs=out_specs, check_vma=False
    )
```

time: 412 us -> 150 us (0.36)
  waiting for transfers between devices: 293 us -> 13.3 us
  Pallas kernels: 0 us -> 33 us
  between operations: 14.7 us -> 1.43 us
  starting transfers between devices: 45.4 us -> 37.4 us
  other arithmetic: 26.7 us -> 32.6 us
    psum x1 -> x0, waiting for transfers between devices: 272 us -> none  [per_device(): weight_total = lax.psum(query_partial + passage_partial, ('batch', 'mp'))]
    pallas_call x0 -> x1, Pallas kernels: none -> 33 us  [reduce_all(): pl.pallas_call(reduce_kernel, out_shape=jax.ShapeDtypeStruct((rows, dim),...]
    ppermute x6 -> x8, starting transfers between devices: 45.3 us -> 37.4 us  [shifted(): lax.ppermute(block, 'batch', [(i, (i + distance) % count) for i in range(...]
    ppermute x6 -> x8, waiting for transfers between devices: 20.9 us -> 13.3 us  [shifted(): lax.ppermute(block, 'batch', [(i, (i + distance) % count) for i in range(...]
  transfers between devices with their start and end apart: 7 -> 8, of which waited for: 5 -> 5; matrix products, arithmetic and copies ran while one was open for 6% -> 10% of each run, Pallas kernels for 0% -> 0%
where the time goes in v1:
time: 150 us; the launch traced here: 149 us
  starting transfers between devices  37.4 us (25%)
  Pallas kernels  33 us (22%)
  other arithmetic  32.6 us (22%)
  local copies, waits for them, and re-layouts  16.6 us (11%)
  matrix products  15 us (10%)
  waiting for transfers between devices  13.3 us (9%)
    ppermute x8, starting transfers between devices, shifted(): lax.ppermute(block, 'batch', [(i, (i + distance) % count) for i in range(...  37.4 us
    pallas_call x1, Pallas kernels, reduce_all(): pl.pallas_call(reduce_kernel, out_shape=jax.ShapeDtypeStruct((rows, dim),...  33 us
    ppermute x8, waiting for transfers between devices, shifted(): lax.ppermute(block, 'batch', [(i, (i + distance) % count) for i in range(...  13.3 us
    mul x3, local copies, waits for them, and re-layouts, candidate_block(): logits = jnp.where(passage_valid[None, None], sims * inner_scale, -jnp.inf)  6.81 us
    convert_element_type x1, other arithmetic, per_device(): grad_sim = (outer_scale * dscores[:, None, :, None] * keeps[b][:, :, None...  6.47 us
    reduce_sum x2, other arithmetic, candidate_block(): totals = jnp.sum(powers, axis=-1, keepdims=True)  5.75 us
    dot_general x3, matrix products, candidate_block(): jnp.dot(query_embed, passage_embed.T, preferred_element_type=jnp.float32)  5.05 us
    unnamed x77, local copies, waits for them, and re-layouts  3.69 us
  transfers between devices with their start and end apart: 8, of which 5 were waited for; matrix products, arithmetic and copies ran while one was open for 10% of the time, Pallas kernels for 0%

profile of v1, /device:TPU:1, one launch (start us, length us, event | category | flops | bytes accessed | tf_op | source)
XLA Modules:
  0.0 149.3 jit_solution(16457893030268752499)
XLA Ops:
  1.4 1.4 multiply_reduce_fusion.6
  3.1 8.3 %collective-permute-start.2 = (bf16[264,128]{1,0:T(8,128)(2,1)S(1)}, bf16[264,128]{1,0:T(8,128)(2,1)S(1)}, u32[]{:S(2)}, u32[]{:S(2)}) collective-permute-start(bf16[264,128]{1,0:T(8,128)(2,1)S(1)} %pad_maximum_fusion), channel_id=1, source_target_pairs={{0,8},{4,12},{8,16},{12,20},{16,24},{20,28},{24,32},{28,36},{32,40... | collective-permute-start | bytes 202760 | tf_op jit(solution)/shard_map/ppermute | solution.py:22
  11.4 2.4 %collective-permute-start = (bf16[264,128]{1,0:T(8,128)(2,1)S(1)}, bf16[264,128]{1,0:T(8,128)(2,1)S(1)}, u32[]{:S(2)}, u32[]{:S(2)}) collective-permute-start(bf16[264,128]{1,0:T(8,128)(2,1)S(1)} %pad_maximum_fusion), channel_id=1, source_target_pairs={{0,4},{4,8},{8,12},{12,16},{16,20},{20,24},{24,28},{28,32},{32,36}... | collective-permute-start | bytes 202760 | tf_op jit(solution)/shard_map/ppermute | solution.py:22
  16.5 1.7 %multiply_reduce_fusion.1 = (f32[1280]{0:T(1024)S(1)}, f32[1280,128]{0,1:T(8,128)S(1)}) fusion(bf16[1280,768]{1,0:T(8,128)(2,1)S(1)} %copy-done, bf16[768,128]{1,0:T(8,128)(2,1)} %param.8), kind=kOutput, calls=%fused_computation.35 | convolution fusion | flops 251984640 | bytes 2823168 | tf_op jit(solution)/shard_map/dot_general | solution.py:113
  19.6 1.6 %mul.227 = f32[8,32,10,128]{3,2,1,0:T(8,128)} reshape(f32[256,1280]{1,0:T(8,128)S(1)} %convolution_multiply_fusion.2) | data formatting | bytes 2621440 | tf_op jit(solution)/shard_map/mul | solution.py:123
  21.2 2.7 %collective-permute-done.2 = bf16[264,128]{1,0:T(8,128)(2,1)S(1)} collective-permute-done((bf16[264,128]{1,0:T(8,128)(2,1)S(1)}, bf16[264,128]{1,0:T(8,128)(2,1)S(1)}, u32[]{:S(2)}, u32[]{:S(2)}) %collective-permute-start.2) | collective-permute-done | bytes 67616 | tf_op jit(solution)/shard_map/ppermute | solution.py:22
  25.3 1.9 %collective-permute-done = bf16[264,128]{1,0:T(8,128)(2,1)S(1)} collective-permute-done((bf16[264,128]{1,0:T(8,128)(2,1)S(1)}, bf16[264,128]{1,0:T(8,128)(2,1)S(1)}, u32[]{:S(2)}, u32[]{:S(2)}) %collective-permute-start) | collective-permute-done | bytes 67616 | tf_op jit(solution)/shard_map/ppermute | solution.py:22
  28.0 2.3 %convolution_multiply_fusion.1 = f32[256,1280]{1,0:T(8,128)} fusion(bf16[1280,128]{0,1:T(8,128)(2,1)} %copy-done.5, bf16[264,128]{1,0:T(8,128)(2,1)S(1)} %collective-permute-done), kind=kOutput, calls=%fused_computation.2 | convolution fusion | flops 84213760 | bytes 1703936 | tf_op jit(solution)/shard_map/dot_general | solution.py:121
  30.3 2.6 %mul.234 = f32[8,32,10,128]{3,2,1,0:T(8,128)} reshape(f32[256,1280]{1,0:T(8,128)} %convolution_multiply_fusion.1) | data formatting | bytes 2621440 | tf_op jit(solution)/shard_map/mul | solution.py:123
  32.9 2.4 %convolution_multiply_fusion = f32[256,1280]{1,0:T(8,128)} fusion(bf16[1280,128]{0,1:T(8,128)(2,1)} %copy-done.5, bf16[264,128]{1,0:T(8,128)(2,1)S(1)} %collective-permute-done.2), kind=kOutput, calls=%fused_computation.1 | convolution fusion | flops 84213760 | bytes 1703936 | tf_op jit(solution)/shard_map/dot_general | solution.py:121
  35.3 2.6 %mul.240 = f32[8,32,10,128]{3,2,1,0:T(8,128)} reshape(f32[256,1280]{1,0:T(8,128)} %convolution_multiply_fusion) | data formatting | bytes 2621440 | tf_op jit(solution)/shard_map/mul | solution.py:123
  37.9 3.5 %select_reduce_fusion.1 = (f32[8,32,10]{2,1,0:T(8,128)S(1)}, f32[8,32,10]{2,1,0:T(8,128)S(1)}) fusion(f32[8,32,10,128]{3,2,1,0:T(8,128)} %mul.234, pred[10,128]{1,0:T(8,128)(4,1)S(1)} %iota_compare_fusion, f32[8,32,10,128]{3,2,1,0:T(8,128)} %mul.227), kind=kLoop, calls=%fused_computation.10 | loop fusion | flops 1305600 | bytes 2643200 | tf_op jit(solution)/shard_map/reduce_max | solution.py:124
  41.5 4.4 %exponential_reduce_fusion.1 = (f32[8,32,10]{2,1,0:T(8,128)S(1)}, f32[8,32,10]{2,1,0:T(8,128)S(1)}, f32[8,32,10]{2,1,0:T(8,128)S(1)}) fusion(f32[8,32,10,128]{3,2,1,0:T(8,128)} %mul.234, f32[8,32,10]{2,1,0:T(8,128)S(1)} %get-tuple-element.9, pred[10,128]{1,0:T(8,128)(4,1)S(1)} %iota_compare_fusion, f32[8,32,10,128]{3,2,1,0:T(8,128)S(1)} %copy-done.2, ...), kind=kLoop, calls=%fused_computation.7 | loop fusion | flops 2613760 | bytes 3984640 | tf_op jit(solution)/shard_map/reduce_sum | solution.py:126
  46.0 1.3 exponential_reduce_fusion
  48.3 6.0 %collective-permute-start.1 = (f32[8,10]{1,0:T(8,128)S(1)}, f32[8,10]{1,0:T(8,128)}, u32[]{:S(2)}, u32[]{:S(2)}) collective-permute-start(f32[8,10]{1,0:T(8,128)S(1)} %broadcast_multiply_fusion.4), channel_id=1, source_target_pairs={{0,508},{4,0},{8,4},{12,8},{16,12},{20,16},{24,20},{28,24},{32,28}... | collective-permute-start | bytes 968 | tf_op jit(solution)/shard_map/ppermute | solution.py:22
  54.3 7.3 %collective-permute-start.3 = (f32[8,10]{1,0:T(8,128)}, f32[8,10]{1,0:T(8,128)}, u32[]{:S(2)}, u32[]{:S(2)}) collective-permute-start(f32[8,10]{1,0:T(8,128)} %broadcast_multiply_fusion.3), channel_id=1, source_target_pairs={{0,504},{4,508},{8,0},{12,4},{16,8},{20,12},{24,16},{28,20},{32,24... | collective-permute-start | bytes 968 | tf_op jit(solution)/shard_map/ppermute | solution.py:22
  61.6 1.2 select_reduce_fusion.3
  63.5 1.3 reduce_max.79
  64.8 1.3 reduce_max.82
  67.6 1.2 fusion.26
  69.6 1.9 %collective-permute-start.6 = (f32[8,1]{0,1:T(1,128)S(1)}, f32[8,1]{0,1:T(1,128)S(1)}, u32[]{:S(2)}, u32[]{:S(2)}) collective-permute-start(f32[8,1]{0,1:T(1,128)S(1)} %bitcast.104), channel_id=1, source_target_pairs={{0,8},{4,12},{8,16},{12,20},{16,24},{20,28},{24,32},{28,36},{32,40... | collective-permute-start | bytes 104 | tf_op jit(solution)/shard_map/ppermute | solution.py:22
  71.5 2.1 %collective-permute-start.4 = (f32[8,1]{0,1:T(1,128)S(1)}, f32[8,1]{0,1:T(1,128)S(1)}, u32[]{:S(2)}, u32[]{:S(2)}) collective-permute-start(f32[8,1]{0,1:T(1,128)S(1)} %bitcast.105), channel_id=1, source_target_pairs={{0,4},{4,8},{8,12},{12,16},{16,20},{20,24},{24,28},{28,32},{32,36}... | collective-permute-start | bytes 104 | tf_op jit(solution)/shard_map/ppermute | solution.py:22
  74.4 7.6 %collective-permute-done.6 = f32[8,1]{0,1:T(1,128)S(1)} collective-permute-done((f32[8,1]{0,1:T(1,128)S(1)}, f32[8,1]{0,1:T(1,128)S(1)}, u32[]{:S(2)}, u32[]{:S(2)}) %collective-permute-start.6) | collective-permute-done | bytes 64 | tf_op jit(solution)/shard_map/ppermute | solution.py:22
  89.8 6.5 %fusion.4 = (bf16[256,1280]{1,0:T(8,128)(2,1)S(1)}, bf16[256,1280]{1,0:T(8,128)(2,1)S(1)}, bf16[256,1280]{1,0:T(8,128)(2,1)S(1)}) fusion(f32[32,8,10,128]{3,2,1,0:T(8,128)S(1)} %bitcast.102, f32[32,8,10,128]{3,2,1,0:T(8,128)S(1)} %bitcast.103, f32[32,8,10,128]{3,2,1,0:T(8,128)S(1)} %bitcast.97, f32[256,1280]{1,0:T(8,128)S(1)} %copy-done.3, ...), kind=kLoop, calls=%fused_computation.19 | loop fusion | flops 4915200 | bytes 17696000 | tf_op jit(solution)/shard_map/convert_element_type | solution.py:186
  97.0 7.4 %collective-permute-start.7 = (bf16[256,128]{1,0:T(8,128)(2,1)S(1)}, bf16[256,128]{1,0:T(8,128)(2,1)S(1)}, u32[]{:S(2)}, u32[]{:S(2)}) collective-permute-start(bf16[256,128]{1,0:T(8,128)(2,1)S(1)} %convolution_convert_fusion.2), channel_id=1, source_target_pairs={{0,504},{4,508},{8,0},{12,4},{16,8},{20,12},{24,16},{28,20},{32,24... | collective-permute-start | bytes 196616 | tf_op jit(solution)/shard_map/ppermute | solution.py:22
  104.5 2.0 %collective-permute-start.5 = (bf16[256,128]{1,0:T(8,128)(2,1)S(1)}, bf16[256,128]{1,0:T(8,128)(2,1)S(1)}, u32[]{:S(2)}, u32[]{:S(2)}) collective-permute-start(bf16[256,128]{1,0:T(8,128)(2,1)S(1)} %convolution_convert_fusion.3), channel_id=1, source_target_pairs={{0,508},{4,0},{8,4},{12,8},{16,12},{20,16},{24,20},{28,24},{32,28}... | collective-permute-start | bytes 196616 | tf_op jit(solution)/shard_map/ppermute | solution.py:22
  108.1 2.0 %convolution_convert_fusion = bf16[1280,768]{1,0:T(8,128)(2,1)} fusion(bf16[1280,128]{0,1:T(8,128)(2,1)S(1)} %divide_convert_fusion, bf16[768,128]{1,0:T(8,128)(2,1)S(1)} %copy-done.9), kind=kOutput, calls=%fused_computation | convolution fusion | flops 252641280 | bytes 2490368 | tf_op jit(solution)/shard_map/dot_general | solution.py:193
  110.1 1.0 collective-permute-done.5
  112.0 1.0 convolution_convert_fusion.1
  113.0 1.5 %fusion.10.src = bf16[768,128]{1,0:T(8,128)(2,1)} fusion(f32[128,768]{0,1:T(8,128)S(1)} %fusion.28, bf16[1280,128]{0,1:T(8,128)(2,1)S(1)} %divide_convert_fusion, bf16[1280,768]{1,0:T(8,128)(2,1)S(1)} %copy-done), kind=kOutput, calls=%fused_computation.30 | convolution fusion | flops 251854848 | bytes 2883584 | tf_op jit(solution)/shard_map/dot_general | solution.py:140
  114.5 33.0 %shard_map.93 = f32[768,128]{1,0:T(8,128)} custom-call(bf16[768,128]{1,0:T(8,128)(2,1)} %fusion.10.src), custom_call_target="tpu_custom_call" | custom-call | tf_op jit(solution)/shard_map/pallas_call | solution.py:96
  147.5 1.8 %copy.38 = f32[768,128]{1,0:T(8,128)} copy(f32[768,128]{1,0:T(8,128)} %shard_map.93) | data formatting | bytes 786432
  (129 shorter events, 22.5 us)
Async XLA Ops:
  0.6 15.8 %copy-start = (bf16[1280,768]{1,0:T(8,128)(2,1)S(1)}, bf16[1280,768]{1,0:T(8,128)(2,1)}, u32[]{:S(2)}) copy-start(bf16[1280,768]{1,0:T(8,128)(2,1)} %param.7) | copy-start | bytes 5898244
  2.8 13.0 %copy-start.17 = (f32[256,128]{1,0:T(8,128)}, f32[256,128]{1,0:T(8,128)S(1)}, u32[]{:S(2)}) copy-start(f32[256,128]{1,0:T(8,128)S(1)} %get-tuple-element.22) | copy-start | bytes 393220
  2.8 11.6 %copy-start.31 = (f32[256]{0:T(256)}, f32[256]{0:T(256)S(1)}, u32[]{:S(2)}) copy-start(f32[256]{0:T(256)S(1)} %add_sqrt_fusion.1) | copy-start | bytes 3076
  3.0 15.3 %copy-start.21 = (bf16[256,128]{1,0:T(8,128)(2,1)}, bf16[256,128]{1,0:T(8,128)(2,1)S(1)}, u32[]{:S(2)}) copy-start(bf16[256,128]{1,0:T(8,128)(2,1)S(1)} %fusion.24) | copy-start | bytes 196612
  3.1 20.8 %collective-permute-start.2 = (bf16[264,128]{1,0:T(8,128)(2,1)S(1)}, bf16[264,128]{1,0:T(8,128)(2,1)S(1)}, u32[]{:S(2)}, u32[]{:S(2)}) collective-permute-start(bf16[264,128]{1,0:T(8,128)(2,1)S(1)} %pad_maximum_fusion), channel_id=1, source_target_pairs={{0,8},{4,12},{8,16},{12,20},{16,24},{20,28},{24,32},{28,36},{32,40... | collective-permute-start | bytes 202760 | tf_op jit(solution)/shard_map/ppermute | solution.py:22
  11.4 15.8 %collective-permute-start = (bf16[264,128]{1,0:T(8,128)(2,1)S(1)}, bf16[264,128]{1,0:T(8,128)(2,1)S(1)}, u32[]{:S(2)}, u32[]{:S(2)}) collective-permute-start(bf16[264,128]{1,0:T(8,128)(2,1)S(1)} %pad_maximum_fusion), channel_id=1, source_target_pairs={{0,4},{4,8},{8,12},{12,16},{16,20},{20,24},{24,28},{28,32},{32,36}... | collective-permute-start | bytes 202760 | tf_op jit(solution)/shard_map/ppermute | solution.py:22
  23.9 9.1 %copy-start.25 = (bf16[264,128]{1,0:T(8,128)(2,1)}, bf16[264,128]{1,0:T(8,128)(2,1)S(1)}, u32[]{:S(2)}) copy-start(bf16[264,128]{1,0:T(8,128)(2,1)S(1)} %collective-permute-done.2) | copy-start | bytes 202756
  27.2 5.7 %copy-start.23 = (bf16[264,128]{1,0:T(8,128)(2,1)}, bf16[264,128]{1,0:T(8,128)(2,1)S(1)}, u32[]{:S(2)}) copy-start(bf16[264,128]{1,0:T(8,128)(2,1)S(1)} %collective-permute-done) | copy-start | bytes 202756
  27.3 5.6 %copy-start.34 = (f32[8]{0:T(128)}, f32[8]{0:T(128)S(1)}, u32[]{:S(2)}) copy-start(f32[8]{0:T(128)S(1)} %convert_reduce_fusion.1) | copy-start | bytes 100
  37.9 3.6 %copy-start.1 = (f32[8,32,10,128]{3,2,1,0:T(8,128)S(1)}, f32[8,32,10,128]{3,2,1,0:T(8,128)}, u32[]{:S(2)}) copy-start(f32[8,32,10,128]{3,2,1,0:T(8,128)} %mul.227) | copy-start | bytes 3932164
  37.9 3.6 %copy-start.2 = (f32[8,32,10,128]{3,2,1,0:T(8,128)S(1)}, f32[8,32,10,128]{3,2,1,0:T(8,128)}, u32[]{:S(2)}) copy-start(f32[8,32,10,128]{3,2,1,0:T(8,128)} %mul.240) | copy-start | bytes 3932164
  46.0 2.2 %copy-start.13 = (f32[8,32,10]{2,1,0:T(8,128)}, f32[8,32,10]{2,1,0:T(8,128)S(1)}, u32[]{:S(2)}) copy-start(f32[8,32,10]{2,1,0:T(8,128)S(1)} %get-tuple-element.6) | copy-start | bytes 30724
  46.0 2.3 %copy-start.15 = (f32[8,32,10]{2,1,0:T(8,128)}, f32[8,32,10]{2,1,0:T(8,128)S(1)}, u32[]{:S(2)}) copy-start(f32[8,32,10]{2,1,0:T(8,128)S(1)} %get-tuple-element.8) | copy-start | bytes 30724
  46.0 2.2 %copy-start.30 = (f32[8,32]{1,0:T(8,128)S(1)}, f32[8,32]{1,0:T(8,128)}, u32[]{:S(2)}) copy-start(f32[8,32]{1,0:T(8,128)} %fusion.20) | copy-start | bytes 3076
  46.0 15.6 %copy-start.37 = (s32[8]{0:T(128)S(1)}, s32[8]{0:T(128)}, u32[]{:S(2)}) copy-start(s32[8]{0:T(128)} %param.11) | copy-start | bytes 100
  46.0 16.8 %copy-start.35 = (f32[8]{0:T(128)S(1)}, f32[8]{0:T(128)}, u32[]{:S(2)}) copy-start(f32[8]{0:T(128)} %copy-done.34) | copy-start | bytes 100
  47.6 14.0 %copy-start.27 = (f32[8,10]{1,0:T(8,128)}, f32[8,10]{1,0:T(8,128)S(1)}, u32[]{:S(2)}) copy-start(f32[8,10]{1,0:T(8,128)S(1)} %get-tuple-element.28) | copy-start | bytes 964
  48.3 15.2 %collective-permute-start.1 = (f32[8,10]{1,0:T(8,128)S(1)}, f32[8,10]{1,0:T(8,128)}, u32[]{:S(2)}, u32[]{:S(2)}) collective-permute-start(f32[8,10]{1,0:T(8,128)S(1)} %broadcast_multiply_fusion.4), channel_id=1, source_target_pairs={{0,508},{4,0},{8,4},{12,8},{16,12},{20,16},{24,20},{28,24},{32,28}... | collective-permute-start | bytes 968 | tf_op jit(solution)/shard_map/ppermute | solution.py:22
  54.3 10.5 %collective-permute-start.3 = (f32[8,10]{1,0:T(8,128)}, f32[8,10]{1,0:T(8,128)}, u32[]{:S(2)}, u32[]{:S(2)}) collective-permute-start(f32[8,10]{1,0:T(8,128)} %broadcast_multiply_fusion.3), channel_id=1, source_target_pairs={{0,504},{4,508},{8,0},{12,4},{16,8},{20,12},{24,16},{28,20},{32,24... | collective-permute-start | bytes 968 | tf_op jit(solution)/shard_map/ppermute | solution.py:22
  69.6 12.4 %collective-permute-start.6 = (f32[8,1]{0,1:T(1,128)S(1)}, f32[8,1]{0,1:T(1,128)S(1)}, u32[]{:S(2)}, u32[]{:S(2)}) collective-permute-start(f32[8,1]{0,1:T(1,128)S(1)} %bitcast.104), channel_id=1, source_target_pairs={{0,8},{4,12},{8,16},{12,20},{16,24},{20,28},{24,32},{28,36},{32,40... | collective-permute-start | bytes 104 | tf_op jit(solution)/shard_map/ppermute | solution.py:22
  71.5 10.6 %collective-permute-start.4 = (f32[8,1]{0,1:T(1,128)S(1)}, f32[8,1]{0,1:T(1,128)S(1)}, u32[]{:S(2)}, u32[]{:S(2)}) collective-permute-start(f32[8,1]{0,1:T(1,128)S(1)} %bitcast.105), channel_id=1, source_target_pairs={{0,4},{4,8},{8,12},{12,16},{16,20},{20,24},{24,28},{28,32},{32,36}... | collective-permute-start | bytes 104 | tf_op jit(solution)/shard_map/ppermute | solution.py:22
  88.1 1.7 %copy-start.4 = (f32[256,1280]{1,0:T(8,128)S(1)}, f32[256,1280]{1,0:T(8,128)}, u32[]{:S(2)}) copy-start(f32[256,1280]{1,0:T(8,128)} %convolution_multiply_fusion) | copy-start | bytes 3932164
  89.8 6.5 %copy-start.6 = (bf16[1280,128]{0,1:T(8,128)(2,1)S(1)}, bf16[1280,128]{0,1:T(8,128)(2,1)}, u32[]{:S(2)}) copy-start(bf16[1280,128]{0,1:T(8,128)(2,1)} %copy-done.5) | copy-start | bytes 983044
  96.3 10.2 %copy-start.22 = (bf16[256,128]{1,0:T(8,128)(2,1)S(1)}, bf16[256,128]{1,0:T(8,128)(2,1)}, u32[]{:S(2)}) copy-start(bf16[256,128]{1,0:T(8,128)(2,1)} %copy-done.21) | copy-start | bytes 196612
  96.3 10.5 %copy-start.24 = (bf16[264,128]{1,0:T(8,128)(2,1)S(1)}, bf16[264,128]{1,0:T(8,128)(2,1)}, u32[]{:S(2)}) copy-start(bf16[264,128]{1,0:T(8,128)(2,1)} %copy-done.23) | copy-start | bytes 202756
  97.0 10.1 %copy-start.8 = (f32[1280,128]{0,1:T(8,128)S(1)}, f32[1280,128]{0,1:T(8,128)}, u32[]{:S(2)}) copy-start(f32[1280,128]{0,1:T(8,128)} %copy-done.7) | copy-start | bytes 1966084
  97.0 10.1 %copy-start.26 = (bf16[264,128]{1,0:T(8,128)(2,1)S(1)}, bf16[264,128]{1,0:T(8,128)(2,1)}, u32[]{:S(2)}) copy-start(bf16[264,128]{1,0:T(8,128)(2,1)} %copy-done.25) | copy-start | bytes 202756
  97.0 13.0 %collective-permute-start.7 = (bf16[256,128]{1,0:T(8,128)(2,1)S(1)}, bf16[256,128]{1,0:T(8,128)(2,1)S(1)}, u32[]{:S(2)}, u32[]{:S(2)}) collective-permute-start(bf16[256,128]{1,0:T(8,128)(2,1)S(1)} %convolution_convert_fusion.2), channel_id=1, source_target_pairs={{0,504},{4,508},{8,0},{12,4},{16,8},{20,12},{24,16},{28,20},{32,24... | collective-permute-start | bytes 196616 | tf_op jit(solution)/shard_map/ppermute | solution.py:22
  104.5 6.6 %collective-permute-start.5 = (bf16[256,128]{1,0:T(8,128)(2,1)S(1)}, bf16[256,128]{1,0:T(8,128)(2,1)S(1)}, u32[]{:S(2)}, u32[]{:S(2)}) collective-permute-start(bf16[256,128]{1,0:T(8,128)(2,1)S(1)} %convolution_convert_fusion.3), channel_id=1, source_target_pairs={{0,508},{4,0},{8,4},{12,8},{16,12},{20,16},{24,20},{28,24},{32,28}... | collective-permute-start | bytes 196616 | tf_op jit(solution)/shard_map/ppermute | solution.py:22
  107.5 3.6 %copy-start.18 = (f32[256,128]{1,0:T(8,128)S(1)}, f32[256,128]{1,0:T(8,128)}, u32[]{:S(2)}) copy-start(f32[256,128]{1,0:T(8,128)} %copy-done.17) | copy-start | bytes 393220
  107.5 3.6 %copy-start.32 = (f32[256]{0:T(256)S(1)}, f32[256]{0:T(256)}, u32[]{:S(2)}) copy-start(f32[256]{0:T(256)} %copy-done.31) | copy-start | bytes 3076
  108.1 3.6 %copy-start.12 = (bf16[256,768]{1,0:T(8,128)(2,1)S(1)}, bf16[256,768]{1,0:T(8,128)(2,1)}, u32[]{:S(2)}) copy-start(bf16[256,768]{1,0:T(8,128)(2,1)} %param.6) | copy-start | bytes 1179652
  (14 other events, 17.5 us)

commit v2 on v1

v2 whole, which is shorter than its diff:
```python
import jax
import jax.numpy as jnp
from jax import lax
from jax.experimental import pallas as pl
from jax.experimental.pallas import tpu as pltpu
from jax.sharding import PartitionSpec as P

inner_scale = 128.0
outer_scale = 8.0
loss_scale = 32.0
norm_eps = 1e-06
hidden_out = -1e30

NX, NZ, NYH, NMP = 4, 8, 4, 4
NG = NYH * NMP
NB = NX * NZ * NYH
MESH = pl.DeviceIdType.MESH
F32 = jnp.float32
BF16 = jnp.bfloat16
QN, QT, PN, PT = 8, 32, 10, 128
QR, PR, DIM, HID = QN * QT, PN * PT, 128, 768
TAIL = 16
HOPS = (1, 2, -1, -2)
CHUNK = 256


def exact_iota(shape, axis):
    return lax.broadcasted_iota(jnp.int32, shape, axis)


def nt_dot(left, right):
    return lax.dot_general(left, right, (((1,), (1,)), ((), ())), preferred_element_type=F32)


def log_sum(rows):
    top = jnp.maximum(jnp.maximum(rows[0], rows[1]), rows[2])
    return top + jnp.log(jnp.exp(rows[0] - top) + jnp.exp(rows[1] - top) + jnp.exp(rows[2] - top))


def step_kernel(
    qlen, plen, pos, qh_any, ph_any, proj_any,
    loss_out, ppre_out, qpre_out, total_out,
    qh, ph, proj, qbuf, qunit, qrad, paug, ptr, punit, prad, power, gsim,
    tops, tots, score, keeps, coef, member, lse_own, lse_in, tq_out, tq_in,
    ppre_t, ppart, src, r1, b2, b3, g4,
    in_sem, qs, qr, ls, lr, ts, tr, s1, q1, s2, q2, s3, q3, s4, q4,
):
    bi = lax.axis_index("batch")
    mi = lax.axis_index("mp")
    yh = bi % NYH
    z = (bi // NYH) % NZ
    x = bi // (NYH * NZ)
    g = yh * NMP + mi
    rows = HID // NG

    def ring_peer(hop):
        return ((bi + (hop + NB)) % NB, mi)

    def group_peer(o):
        j = (g + o) % NG
        return j, (bi - yh + j // NMP, j % NMP)

    def z_peer(o):
        j = (z + o) % NZ
        return j, (x * (NZ * NYH) + j * NYH + yh, mi)

    def x_peer(o):
        j = (x + o) % NX
        return j, (j * (NZ * NYH) + z * NYH + yh, mi)

    get_proj = pltpu.make_async_copy(proj_any, proj, in_sem.at[0])
    get_qh = pltpu.make_async_copy(qh_any, qh, in_sem.at[1])
    get_ph = pltpu.make_async_copy(ph_any, ph, in_sem.at[2])
    get_proj.start()
    get_qh.start()
    get_ph.start()

    barrier = pltpu.get_barrier_semaphore()
    for hop in HOPS:
        pl.semaphore_signal(barrier, inc=1, device_id=ring_peer(hop), device_id_type=MESH)
    for count, peer in ((NG, group_peer), (NZ, z_peer), (NX, x_peer)):
        @pl.loop(1, count)
        def _(o):
            pl.semaphore_signal(barrier, inc=1, device_id=peer(o)[1], device_id_type=MESH)

    lane = exact_iota((1, QR), 1)
    keep = jnp.zeros((1, QR), F32)
    for q in range(QN):
        token = lane - q * QT
        keep = jnp.where((token >= 0) & (token < qlen[q]), 1.0, keep)
    tail_row = exact_iota((TAIL, QR), 0)
    qbuf[0, DIM:DIM + TAIL, :] = jnp.where(
        tail_row == 0, 1.0, jnp.where(tail_row == 1, keep, 0.0)).astype(BF16)
    for b in range(3):
        qbuf[b, DIM + TAIL:, :] = jnp.zeros((QR - DIM - TAIL, QR), BF16)

    get_proj.wait()
    get_qh.wait()
    before = jnp.dot(qh[...], proj[...], preferred_element_type=F32).T
    radius = jnp.sqrt(jnp.sum(before * before, axis=0, keepdims=True) + norm_eps)
    unit = before / radius
    qunit[...] = unit
    qrad[...] = radius
    qbuf[0, :DIM, :] = unit.astype(BF16)

    pl.semaphore_wait(barrier, 4 + NG + NZ + NX - 3)

    def send_query(b):
        part = pl.ds(0, DIM + TAIL)
        return pltpu.make_async_remote_copy(
            src_ref=qbuf.at[0, part], dst_ref=qbuf.at[b, part], send_sem=qs.at[b - 1],
            recv_sem=qr.at[b - 1], device_id=ring_peer(b), device_id_type=MESH)

    send_query(1).start()
    send_query(2).start()

    member[...] = jnp.where(
        exact_iota((QR, QR), 0) // QT == exact_iota((QR, QR), 1) // QT, 1.0, 0.0)
    tops[...] = jnp.zeros(tops.shape, F32)
    tots[...] = jnp.ones(tots.shape, F32)

    @pl.loop(0, PN)
    def _(c):
        spot = pl.ds(pl.multiple_of(c * PT, PT), PT)
        outside = (exact_iota((PT, DIM), 0) >= plen[c]) & (exact_iota((PT, DIM), 1) == 0)
        paug[spot, DIM:] = jnp.where(outside, hidden_out, 0.0).astype(BF16)

    get_ph.wait()

    @pl.loop(0, PR // CHUNK)
    def _(r):
        spot = pl.ds(pl.multiple_of(r * CHUNK, CHUNK), CHUNK)
        before = jnp.dot(ph[spot, :], proj[...], preferred_element_type=F32)
        radius = jnp.sqrt(jnp.sum(before * before, axis=-1, keepdims=True) + norm_eps)
        unit = before / radius
        punit[spot, :] = unit
        prad[spot, :] = radius
        embed = unit.astype(BF16)
        paug[spot, :DIM] = embed * jnp.array(inner_scale, BF16)
        ptr[:, spot] = embed.astype(F32).T.astype(BF16)

    def forward(b):
        power[b] = jnp.dot(paug[...], qbuf[b], preferred_element_type=F32)

        @pl.loop(0, PN)
        def _(c):
            spot = pl.ds(pl.multiple_of(c * PT, PT), PT)
            logits = power[b, spot, :]
            top = jnp.max(logits, axis=0, keepdims=True)
            powers = jnp.exp(logits - top)
            power[b, spot, :] = powers
            tops[b, pl.ds(c, 1), :] = top
            tots[b, pl.ds(c, 1), :] = jnp.sum(powers, axis=0, keepdims=True)

        kept = qbuf[b, DIM:DIM + TAIL, :].astype(F32)[1:2, :]
        keeps[b] = jnp.broadcast_to(kept, (TAIL, QR))
        best = (jnp.log(tots[b]) + tops[b]) * (1.0 / inner_scale)
        scores = outer_scale * jnp.dot(
            best * kept, member[...], preferred_element_type=F32, precision=lax.Precision.HIGHEST)
        scores = jnp.where(exact_iota((TAIL, QR), 0) < PN, scores, hidden_out)
        score[b] = scores
        top = jnp.max(scores, axis=0, keepdims=True)
        total = top + jnp.log(jnp.sum(jnp.exp(scores - top), axis=0, keepdims=True))
        lse_own[pl.ds(b, 1), :] = total
        return total

    def to_grads(b, dscore):
        coef[...] = dscore * keeps[b] * (outer_scale * loss_scale) / tots[b]

        @pl.loop(0, PN)
        def _(c):
            spot = pl.ds(pl.multiple_of(c * PT, PT), PT)
            gsim[b, spot, :] = (power[b, spot, :] * coef[pl.ds(c, 1), :]).astype(BF16)

    def send_grad(b):
        return pltpu.make_async_remote_copy(
            src_ref=tq_out.at[b - 1], dst_ref=tq_in.at[b - 1], send_sem=ts.at[b - 1],
            recv_sem=tr.at[b - 1], device_id=ring_peer(-b), device_id_type=MESH)

    def send_lse(n):
        return pltpu.make_async_remote_copy(
            src_ref=lse_own, dst_ref=lse_in.at[n], send_sem=ls.at[n], recv_sem=lr.at[n],
            device_id=ring_peer(HOPS[n]), device_id_type=MESH)

    lse_own[...] = jnp.zeros(lse_own.shape, F32)
    forward(0)
    own = []
    for b in (1, 2):
        send_query(b).wait_recv()
        own.append(forward(b))
        if b == 2:
            for n in range(4):
                send_lse(n).start()
        to_grads(b, jnp.exp(score[b] - own[b - 1]))
        tq_out[b - 1] = jnp.dot(ptr[...], gsim[b], preferred_element_type=F32).astype(BF16)
        send_grad(b).start()

    for n in range(4):
        send_lse(n).wait_recv()
    totals = (
        log_sum((lse_own[0:1, :], lse_in[2, 1:2, :], lse_in[3, 2:3, :])),
        log_sum((lse_in[0, 0:1, :], lse_own[1:2, :], lse_in[2, 2:3, :])),
        log_sum((lse_in[1, 0:1, :], lse_in[0, 1:2, :], lse_own[2:3, :])),
    )
    place = jnp.zeros((1, QR), jnp.int32)
    for q in range(QN):
        place = jnp.where(lane // QT == q, pos[q], place)
    onehot = jnp.where(exact_iota((TAIL, QR), 0) == place, 1.0, 0.0)
    loss_out[...] = totals[0] - jnp.sum(onehot * score[0], axis=0, keepdims=True)
    for b in range(3):
        dscore = jnp.exp(score[b] - totals[b])
        to_grads(b, dscore - onehot if b == 0 else dscore)
    own_grad = jnp.dot(ptr[...], gsim[0], preferred_element_type=F32)
    qgrad = own_grad

    @pl.loop(0, PR // CHUNK)
    def _(r):
        spot = pl.ds(pl.multiple_of(r * CHUNK, CHUNK), CHUNK)
        grad = nt_dot(gsim[0, spot, :], qbuf[0, :DIM, :])
        grad += nt_dot(gsim[1, spot, :], qbuf[1, :DIM, :])
        grad += nt_dot(gsim[2, spot, :], qbuf[2, :DIM, :])
        unit = punit[spot, :]
        pre = (grad - unit * jnp.sum(unit * grad, axis=-1, keepdims=True)) / prad[spot, :]
        pre = pre.astype(BF16)
        ppre_out[spot, :] = pre
        ppre_t[:, spot] = pre.astype(F32).T.astype(BF16)

    ppart[...] = jnp.dot(ppre_t[...], ph[...], preferred_element_type=F32)

    send_grad(1).wait_recv()
    send_grad(2).wait_recv()
    qgrad += jnp.exp(lse_in[2, 1:2, :] - totals[0]) * tq_in[0].astype(F32)
    qgrad += jnp.exp(lse_in[3, 2:3, :] - totals[0]) * tq_in[1].astype(F32)
    unit = qunit[...]
    pre = (qgrad - unit * jnp.sum(unit * qgrad, axis=0, keepdims=True)) / qrad[...]
    pre = pre.astype(BF16)
    qpre_out[...] = pre
    part = ppart[...] + jnp.dot(pre, qh[...], preferred_element_type=F32)
    for t in range(HID // DIM):
        src[t * DIM:(t + 1) * DIM, :] = part[:, t * DIM:(t + 1) * DIM].astype(BF16)

    def piece(j):
        return pl.ds(pl.multiple_of(j * rows, rows), rows)

    def exchange(count, peer, source, target, mine, send, recv):
        def copy(o):
            j, where = peer(o)
            return pltpu.make_async_remote_copy(
                src_ref=source(j), dst_ref=target(mine), send_sem=send.at[o],
                recv_sem=recv.at[mine], device_id=where, device_id_type=MESH)

        def arrival(o):
            j, where = peer(o)
            return pltpu.make_async_remote_copy(
                src_ref=source(j), dst_ref=target(j), send_sem=send.at[o], recv_sem=recv.at[j],
                device_id=where, device_id_type=MESH)

        @pl.loop(1, count)
        def _(o):
            copy(o).start()

        @pl.loop(1, count)
        def _(o):
            arrival(o).wait_recv()

        def finish():
            @pl.loop(1, count)
            def _(o):
                copy(o).wait_send()

        return finish

    r1[g] = src[piece(g), :]
    done1 = exchange(
        NG, group_peer, lambda j: src.at[piece(j)], lambda j: r1.at[j], g, s1, q1)
    b2[z] = jnp.sum(r1[...].astype(F32), axis=0).astype(BF16)
    done2 = exchange(NZ, z_peer, lambda j: b2.at[z], lambda j: b2.at[j], z, s2, q2)
    b3[x] = jnp.sum(b2[...].astype(F32), axis=0).astype(BF16)
    done3 = exchange(NX, x_peer, lambda j: b3.at[x], lambda j: b3.at[j], x, s3, q3)
    g4[piece(g), :] = jnp.sum(b3[...].astype(F32), axis=0).astype(BF16)
    done4 = exchange(
        NG, group_peer, lambda j: g4.at[piece(g)], lambda j: g4.at[piece(j)], g, s4, q4)
    total_out[...] = g4[...]
    for done in (done1, done2, done3, done4):
        done()
    for b in (1, 2):
        send_query(b).wait_send()
        send_grad(b).wait_send()
    for n in range(4):
        send_lse(n).wait_send()


def run_step(query_lengths, passage_lengths, positives, query_hidden, passage_hidden, projection):
    dma = pltpu.SemaphoreType.DMA
    smem = pl.BlockSpec(memory_space=pltpu.SMEM)
    vmem = pl.BlockSpec(memory_space=pltpu.VMEM)
    hbm = pl.BlockSpec(memory_space=pl.ANY)
    part = HID // NG
    vm = pltpu.VMEM
    return pl.pallas_call(
        step_kernel,
        out_shape=(
            jax.ShapeDtypeStruct((1, QR), F32),
            jax.ShapeDtypeStruct((PR, DIM), BF16),
            jax.ShapeDtypeStruct((DIM, QR), BF16),
            jax.ShapeDtypeStruct((HID, DIM), BF16),
        ),
        in_specs=[smem, smem, smem, hbm, hbm, hbm],
        out_specs=(vmem, vmem, vmem, vmem),
        scratch_shapes=[
            vm((QR, HID), BF16), vm((PR, HID), BF16), vm((HID, DIM), BF16),
            vm((3, QR, QR), BF16), vm((DIM, QR), F32), vm((1, QR), F32),
            vm((PR, 2 * DIM), BF16), vm((DIM, PR), BF16), vm((PR, DIM), F32), vm((PR, 1), F32),
            vm((3, PR, QR), F32), vm((3, PR, QR), BF16),
            vm((3, TAIL, QR), F32), vm((3, TAIL, QR), F32), vm((3, TAIL, QR), F32),
            vm((3, TAIL, QR), F32), vm((TAIL, QR), F32), vm((QR, QR), F32),
            vm((8, QR), F32), vm((4, 8, QR), F32),
            vm((2, DIM, QR), BF16), vm((2, DIM, QR), BF16),
            vm((DIM, PR), BF16), vm((DIM, HID), F32),
            vm((HID, DIM), BF16), vm((NG, part, DIM), BF16), vm((NZ, part, DIM), BF16),
            vm((NX, part, DIM), BF16), vm((HID, DIM), BF16),
            dma((3,)), dma((2,)), dma((2,)), dma((4,)), dma((4,)), dma((2,)), dma((2,)),
            dma((NG,)), dma((NG,)), dma((NZ,)), dma((NZ,)), dma((NX,)), dma((NX,)), dma((NG,)), dma((NG,)),
        ],
        compiler_params=pltpu.CompilerParams(collective_id=0, has_side_effects=True),
    )(query_lengths, passage_lengths, positives, query_hidden, passage_hidden, projection)


def finish_kernel(loss, ppre, qpre, proj, total, loss_out, gq_any, gp_any, gproj, held, sem):
    for q in range(QN):
        loss_out[q] = loss[0, q * QT]

    def copy(r):
        spot = pl.ds(r * CHUNK, CHUNK)
        where = gq_any if r == PR // CHUNK else gp_any.at[spot]
        return pltpu.make_async_copy(held.at[spot], where, sem.at[r])

    for r in range(PR // CHUNK + 1):
        spot = pl.ds(r * CHUNK, CHUNK)
        if r == PR // CHUNK:
            pre = qpre[...].astype(F32).T.astype(BF16)
        else:
            pre = ppre[spot, :]
        held[spot, :] = nt_dot(pre, proj[...]).astype(BF16)
        copy(r).start()
    for t in range(HID // DIM):
        spot = pl.ds(t * DIM, DIM)
        gproj[spot, :] = total[spot, :].astype(F32).T * (1.0 / (NB * NMP))
    for r in range(PR // CHUNK + 1):
        copy(r).wait()


def run_finish(loss, ppre, qpre, projection, total):
    smem = pl.BlockSpec(memory_space=pltpu.SMEM)
    vmem = pl.BlockSpec(memory_space=pltpu.VMEM)
    hbm = pl.BlockSpec(memory_space=pl.ANY)
    return pl.pallas_call(
        finish_kernel,
        out_shape=(
            jax.ShapeDtypeStruct((QN,), F32),
            jax.ShapeDtypeStruct((QR, HID), BF16),
            jax.ShapeDtypeStruct((PR, HID), BF16),
            jax.ShapeDtypeStruct((HID, DIM), F32),
        ),
        in_specs=[smem, vmem, vmem, vmem, vmem],
        out_specs=(smem, hbm, hbm, vmem),
        scratch_shapes=[
            pltpu.VMEM((PR + QR, HID), BF16),
            pltpu.SemaphoreType.DMA((PR // CHUNK + 1,)),
        ],
    )(loss, ppre, qpre, projection, total)


def per_device(query_hidden, passage_hidden, projection, query_lengths, passage_lengths, positives):
    loss, ppre, qpre, total = run_step(
        query_lengths, passage_lengths, positives, query_hidden, passage_hidden, projection)
    return run_finish(loss, ppre, qpre, projection, total)


def solution(mesh):
    in_specs = (
        P(("batch", "mp"), None),
        P(("batch", "mp"), None),
        P(),
        P(("batch", "mp")),
        P(("batch", "mp")),
        P(("batch", "mp")),
    )
    out_specs = (P(("batch", "mp")), P(("batch", "mp"), None), P(("batch", "mp"), None), P())
    return jax.shard_map(
        per_device, mesh=mesh, in_specs=in_specs, out_specs=out_specs, check_vma=False
    )
```

time: 150 us -> 65.4 us (0.44)
  starting transfers between devices: 37.4 us -> 0 us
  other arithmetic: 32.6 us -> 0 us
  Pallas kernels: 33 us -> 64.5 us
  local copies, waits for them, and re-layouts: 16.6 us -> 0 us
  matrix products: 15 us -> 0 us
  waiting for transfers between devices: 13.3 us -> 0 us
    ppermute x8 -> x0, starting transfers between devices: 37.4 us -> none  [shifted(): lax.ppermute(block, 'batch', [(i, (i + distance) % count) for i in range(...]
    pallas_call x1 -> x2, Pallas kernels: 33 us -> 64.5 us  [the longest x1 60.9 us: run_step(): pl.pallas_call(step_kernel, out_shape=(jax.ShapeDtypeStruct((1, QR), F32)...]
    dot_general x15 -> x0, matrix products: 15 us -> none  [the longest x3 5.05 us: candidate_block(): jnp.dot(query_embed, passage_embed.T, preferred_element_type=jnp.float32)]
    ppermute x8 -> x0, waiting for transfers between devices: 13.3 us -> none  [shifted(): lax.ppermute(block, 'batch', [(i, (i + distance) % count) for i in range(...]
    convert_element_type x11 -> x0, other arithmetic: 9.9 us -> none  [the longest x1 6.47 us: per_device(): grad_sim = (outer_scale * dscores[:, None, :, None] * keeps[b][:, :, None...]
    mul x6 -> x0, local copies, waits for them, and re-layouts: 8.61 us -> none  [the longest x3 6.81 us: candidate_block(): logits = jnp.where(passage_valid[None, None], sims * inner_scale, -jnp.inf)]
    reduce_sum x6 -> x0, other arithmetic: 8.12 us -> none  [the longest x2 5.75 us: candidate_block(): totals = jnp.sum(powers, axis=-1, keepdims=True)]
    reduce_max x4 -> x0, other arithmetic: 6.8 us -> none  [the longest x1 3.54 us: candidate_block(): row_top = jnp.max(logits, axis=-1, keepdims=True)]
  transfers between devices with their start and end apart: 8 -> 0, of which waited for: 5 -> 0; matrix products, arithmetic and copies ran while one was open for 10% -> 0% of each run, Pallas kernels for 0% -> 0%
where the time goes in v2:
time: 65.4 us; the launch traced here: 65.2 us
  Pallas kernels  64.5 us (99%)
    pallas_call x1, Pallas kernels, run_step(): pl.pallas_call(step_kernel, out_shape=(jax.ShapeDtypeStruct((1, QR), F32)...  60.9 us
    pallas_call x1, Pallas kernels, run_finish(): pl.pallas_call(finish_kernel, out_shape=(jax.ShapeDtypeStruct((QN,), F32)...  3.67 us

profile of v2, /device:TPU:1, one launch (start us, length us, event | category | flops | bytes accessed | tf_op | source)
XLA Modules:
  0.0 65.2 jit_solution(4219141333997996535)
XLA Ops:
  0.6 60.9 %shard_map.93 = (f32[1,256]{1,0:T(1,128)}, bf16[1280,128]{1,0:T(8,128)(2,1)}, bf16[128,256]{1,0:T(8,128)(2,1)}, bf16[768,128]{1,0:T(8,128)(2,1)}) custom-call(s32[8]{0:T(128)} %qlen.1, s32[10]{0:T(128)} %plen.1, s32[8]{0:T(128)} %pos.1, bf16[256,768]{1,0:T(8,128)(2,1)} %qh_any.1, bf16[1280,768]{1,0:T(8,128)(2,1)} %ph_any.1, bf16[768,128]{1,0:T(8,128)(2,1)} %proj.1), custom_call_target="tpu_custom_call" | custom-call | tf_op jit(solution)/shard_map/pallas_call | solution.py:300
  61.5 3.7 %shard_map.94 = (f32[8]{0:T(128)}, bf16[256,768]{1,0:T(8,128)(2,1)}, bf16[1280,768]{1,0:T(8,128)(2,1)}, f32[768,128]{1,0:T(8,128)}) custom-call(f32[1,256]{1,0:T(1,128)} %get-tuple-element.8.loss, bf16[1280,128]{1,0:T(8,128)(2,1)} %get-tuple-element.9.ppre, bf16[128,256]{1,0:T(8,128)(2,1)} %get-tuple-element.10.qpre, bf16[768,128]{1,0:T(8,128)(2,1)} %proj.1, ...), custom_call_target="tpu_custom_call" | custom-call | tf_op jit(solution)/shard_map/pallas_call | solution.py:357

commit v3 on v2

v3 whole, which is shorter than its diff:
```python
import jax
import jax.numpy as jnp
from jax import lax
from jax.experimental import pallas as pl
from jax.experimental.pallas import tpu as pltpu
from jax.sharding import PartitionSpec as P

inner_scale = 128.0
outer_scale = 8.0
loss_scale = 32.0
norm_eps = 1e-06
hidden_out = -1e30

NX, NZ, NYH, NYL, NC = 4, 8, 4, 2, 2
NMP = NYL * NC
NB = NX * NZ * NYH
MESH = pl.DeviceIdType.MESH
F32 = jnp.float32
BF16 = jnp.bfloat16
QN, QT, PN, PT = 8, 32, 10, 128
QR, PR, DIM, HID = QN * QT, PN * PT, 128, 768
TAIL = 16
HOPS = (1, 2, -1, -2)
CHUNK = 256
UNROLL = 2


def exact_iota(shape, axis):
    return lax.broadcasted_iota(jnp.int32, shape, axis)


def nt_dot(left, right):
    return lax.dot_general(left, right, (((1,), (1,)), ((), ())), preferred_element_type=F32)


def log_sum(rows):
    top = jnp.maximum(jnp.maximum(rows[0], rows[1]), rows[2])
    return top + jnp.log(jnp.exp(rows[0] - top) + jnp.exp(rows[1] - top) + jnp.exp(rows[2] - top))


def turned(here, count):
    order = sorted(range(count), key=lambda a: -min(a, count - a))
    spots = []
    for a in order:
        there = here + a
        spots.append((a, jnp.where(there >= count, there - count, there) if a else here))
    return spots


def step_kernel(
    qlen, plen, pos, qh_any, ph_any, proj_any,
    loss_out, ppre_any, qpre_any, total_out,
    qh, ph, proj, qbuf, qunit, qrad, paug, ptr, punit, prad, power, gsim,
    tops, tots, score, keeps, coef, member, lse_own, lse_in, tq_out, tq_in, qscaled,
    ppre, ppre_t, qpre, ppart, src, a1, a2, a3, b1, b2, b3, c1, c2, c3, gathered,
    in_sem, out_sem, qs, qr, ls, lr, ts, tr, push, pull,
):
    bi = lax.axis_index("batch")
    mi = lax.axis_index("mp")
    yh = lax.rem(bi, NYH)
    up = lax.div(bi, NYH)
    z = lax.rem(up, NZ)
    x = lax.div(up, NZ)
    yl = lax.div(mi, NC)
    core = lax.rem(mi, NC)
    y = yh * NYL + yl
    xz = bi - yh
    cores = turned(core, NC)

    def at_y(spot, side):
        return (xz + lax.div(spot, NYL), lax.rem(spot, NYL) * NC + side)

    def at_z(spot, side):
        return (bi + (spot - z) * NYH, mi + (side - core))

    def at_x(spot, side):
        return (bi + (spot - x) * (NYH * NZ), mi + (side - core))

    def pairs(spots, place):
        return [(spot * NC + side, place(spot, side)) for a, spot in spots for c, side in cores if a or c]

    def lines(spots, place):
        return [(spot, place(spot, core)) for a, spot in spots if a]

    ys, zs, xs = turned(y, NYH * NYL), turned(z, NZ), turned(x, NX)
    y_pairs, z_pairs, x_pairs = pairs(ys, at_y), pairs(zs, at_z), pairs(xs, at_x)
    y_line, z_line, x_line = lines(ys, at_y), lines(zs, at_z), lines(xs, at_x)

    def ring_peer(hop):
        there = bi + hop
        there = jnp.where(there >= NB, there - NB, there) if hop > 0 else jnp.where(there < 0, there + NB, there)
        return (there, mi)

    ring = {hop: ring_peer(hop) for hop in HOPS}

    get_proj = pltpu.make_async_copy(proj_any, proj, in_sem.at[0])
    get_qh = pltpu.make_async_copy(qh_any, qh, in_sem.at[1])
    get_ph = pltpu.make_async_copy(ph_any, ph, in_sem.at[2])
    get_proj.start()
    get_qh.start()
    get_ph.start()

    barrier = pltpu.get_barrier_semaphore()
    everyone = [ring[hop] for hop in HOPS] + [w for _, w in y_pairs + z_pairs + x_pairs]
    for where in everyone:
        pl.semaphore_signal(barrier, inc=1, device_id=where, device_id_type=MESH)

    lane = exact_iota((1, QR), 1)
    keep = jnp.zeros((1, QR), F32)
    for q in range(QN):
        token = lane - q * QT
        keep = jnp.where((token >= 0) & (token < qlen[q]), 1.0, keep)
    tail_row = exact_iota((TAIL, QR), 0)
    qbuf[0, DIM:DIM + TAIL, :] = jnp.where(
        tail_row == 0, 1.0, jnp.where(tail_row == 1, keep, 0.0)).astype(BF16)
    for b in range(3):
        qbuf[b, DIM + TAIL:, :] = jnp.zeros((QR - DIM - TAIL, QR), BF16)

    get_proj.wait()
    get_qh.wait()
    before = jnp.dot(qh[...], proj[...], preferred_element_type=F32).T
    radius = jnp.sqrt(jnp.sum(before * before, axis=0, keepdims=True) + norm_eps)
    inverse = 1.0 / radius
    unit = before * inverse
    qunit[...] = unit
    qrad[...] = inverse
    qbuf[0, :DIM, :] = unit.astype(BF16)

    pl.semaphore_wait(barrier, len(everyone))

    def send_query(b):
        part = pl.ds(0, DIM + TAIL)
        return pltpu.make_async_remote_copy(
            src_ref=qbuf.at[0, part], dst_ref=qbuf.at[b, part], send_sem=qs.at[b - 1],
            recv_sem=qr.at[b - 1], device_id=ring[b], device_id_type=MESH)

    send_query(2).start()
    send_query(1).start()

    member[...] = jnp.where(
        exact_iota((QR, QR), 0) // QT == exact_iota((QR, QR), 1) // QT, 1.0, 0.0).astype(BF16)
    tops[...] = jnp.zeros(tops.shape, F32)
    tots[...] = jnp.ones(tots.shape, F32)

    @pl.loop(0, PN)
    def _(c):
        spot = pl.ds(pl.multiple_of(c * PT, PT), PT)
        outside = (exact_iota((PT, DIM), 0) >= plen[c]) & (exact_iota((PT, DIM), 1) == 0)
        paug[spot, DIM:] = jnp.where(outside, hidden_out, 0.0).astype(BF16)

    get_ph.wait()

    for r in range(PR // CHUNK):
        spot = pl.ds(r * CHUNK, CHUNK)
        before = jnp.dot(ph[spot, :], proj[...], preferred_element_type=F32)
        radius = jnp.sqrt(jnp.sum(before * before, axis=-1, keepdims=True) + norm_eps)
        inverse = 1.0 / radius
        unit = before * inverse
        punit[spot, :] = unit
        prad[spot, :] = inverse
        embed = unit.astype(BF16)
        paug[spot, :DIM] = embed * jnp.array(inner_scale, BF16)
        ptr[:, spot] = embed.astype(F32).T.astype(BF16)

    def forward(b):
        power[b] = jnp.dot(paug[...], qbuf[b], preferred_element_type=F32)

        @pl.loop(0, PN // UNROLL)
        def _(step):
            for k in range(UNROLL):
                c = step * UNROLL + k
                spot = pl.ds(pl.multiple_of(c * PT, PT), PT)
                logits = power[b, spot, :]
                top = jnp.max(logits, axis=0, keepdims=True)
                powers = jnp.exp(logits - top)
                power[b, spot, :] = powers
                tops[b, pl.ds(c, 1), :] = top
                tots[b, pl.ds(c, 1), :] = jnp.sum(powers, axis=0, keepdims=True)

        kept = qbuf[b, DIM:DIM + TAIL, :].astype(F32)[1:2, :]
        keeps[b] = jnp.broadcast_to(kept, (TAIL, QR))
        best = (jnp.log(tots[b]) + tops[b]) * (1.0 / inner_scale) * kept
        high = best.astype(BF16)
        rest = best - high.astype(F32)
        middle = rest.astype(BF16)
        low = (rest - middle.astype(F32)).astype(BF16)
        sums = jnp.dot(
            jnp.concatenate([high, middle, low], axis=0), member[...], preferred_element_type=F32)
        scores = outer_scale * (sums[:TAIL] + (sums[TAIL:2 * TAIL] + sums[2 * TAIL:]))
        scores = jnp.where(exact_iota((TAIL, QR), 0) < PN, scores, hidden_out)
        score[b] = scores
        top = jnp.max(scores, axis=0, keepdims=True)
        total = top + jnp.log(jnp.sum(jnp.exp(scores - top), axis=0, keepdims=True))
        lse_own[pl.ds(b, 1), :] = total
        return total

    def to_grads(b, dscore):
        coef[...] = dscore * keeps[b] * (outer_scale * loss_scale) / tots[b]

        @pl.loop(0, PN // UNROLL)
        def _(step):
            for k in range(UNROLL):
                c = step * UNROLL + k
                spot = pl.ds(pl.multiple_of(c * PT, PT), PT)
                gsim[b, spot, :] = (power[b, spot, :] * coef[pl.ds(c, 1), :]).astype(BF16)

    def send_grad(b):
        return pltpu.make_async_remote_copy(
            src_ref=tq_out.at[b - 1], dst_ref=tq_in.at[b - 1], send_sem=ts.at[b - 1],
            recv_sem=tr.at[b - 1], device_id=ring[-b], device_id_type=MESH)

    def send_lse(n):
        return pltpu.make_async_remote_copy(
            src_ref=lse_own, dst_ref=lse_in.at[n], send_sem=ls.at[n], recv_sem=lr.at[n],
            device_id=ring[HOPS[n]], device_id_type=MESH)

    lse_own[...] = jnp.zeros(lse_own.shape, F32)
    own = [forward(0)]
    for b in (1, 2):
        send_query(b).wait_recv()
        own.append(forward(b))
    for n in range(4):
        send_lse(n).start()
    for b in (2, 1):
        to_grads(b, jnp.exp(score[b] - lse_own[b:b + 1, :]))
        tq_out[b - 1] = jnp.dot(ptr[...], gsim[b], preferred_element_type=F32).astype(BF16)
        send_grad(b).start()

    place = jnp.zeros((1, QR), jnp.int32)
    for q in range(QN):
        place = jnp.where(lane // QT == q, pos[q], place)
    onehot = jnp.where(exact_iota((TAIL, QR), 0) == place, 1.0, 0.0)

    for n in range(4):
        send_lse(n).wait_recv()
    totals = (
        log_sum((lse_own[0:1, :], lse_in[2, 1:2, :], lse_in[3, 2:3, :])),
        log_sum((lse_in[0, 0:1, :], lse_own[1:2, :], lse_in[2, 2:3, :])),
        log_sum((lse_in[1, 0:1, :], lse_in[0, 1:2, :], lse_own[2:3, :])),
    )
    loss_out[...] = totals[0] - jnp.sum(onehot * score[0], axis=0, keepdims=True)
    for b in (1, 2):
        factor = jnp.exp(lse_own[b:b + 1, :] - totals[b])
        qscaled[b - 1] = (qbuf[b, :DIM, :].astype(F32) * factor).astype(BF16)
    to_grads(0, jnp.exp(score[0] - totals[0]) - onehot)

    for r in range(PR // CHUNK):
        spot = pl.ds(r * CHUNK, CHUNK)
        grad = nt_dot(gsim[0, spot, :], qbuf[0, :DIM, :])
        grad += nt_dot(gsim[1, spot, :], qscaled[0])
        grad += nt_dot(gsim[2, spot, :], qscaled[1])
        unit = punit[spot, :]
        pre = (grad - unit * jnp.sum(unit * grad, axis=-1, keepdims=True)) * prad[spot, :]
        pre = pre.astype(BF16)
        ppre[spot, :] = pre
        ppre_t[:, spot] = pre.astype(F32).T.astype(BF16)

    put_ppre = pltpu.make_async_copy(ppre, ppre_any, out_sem.at[0])
    put_ppre.start()
    ppart[...] = jnp.dot(ppre_t[...], ph[...], preferred_element_type=F32)
    qgrad = jnp.dot(ptr[...], gsim[0], preferred_element_type=F32)

    send_grad(1).wait_recv()
    send_grad(2).wait_recv()
    qgrad += jnp.exp(lse_in[2, 1:2, :] - totals[0]) * tq_in[0].astype(F32)
    qgrad += jnp.exp(lse_in[3, 2:3, :] - totals[0]) * tq_in[1].astype(F32)
    unit = qunit[...]
    pre = (qgrad - unit * jnp.sum(unit * qgrad, axis=0, keepdims=True)) * qrad[...]
    pre = pre.astype(BF16)
    qpre[...] = pre
    part = ppart[...] + jnp.dot(pre, qh[...], preferred_element_type=F32)
    for t in range(HID // DIM):
        src[t * DIM:(t + 1) * DIM, :] = part[:, t * DIM:(t + 1) * DIM].astype(BF16)
    put_qpre = pltpu.make_async_copy(qpre, qpre_any, out_sem.at[1])

    def piece(first, size, j):
        return pl.ds(pl.multiple_of(first + j * size, size), size)

    def start(stage, peers, source, target, mine):
        for j, where in peers:
            pltpu.make_async_remote_copy(
                src_ref=source(j), dst_ref=target(mine), send_sem=push.at[stage],
                recv_sem=pull.at[stage], device_id=where, device_id_type=MESH).start()

    def bulk(stage, peers, whole):
        return pltpu.make_async_remote_copy(
            src_ref=whole, dst_ref=whole, send_sem=push.at[stage], recv_sem=pull.at[stage],
            device_id=peers[0][1], device_id_type=MESH)

    def added(box):
        return jnp.sum(box[...].astype(F32), axis=0).astype(BF16)

    plan = []
    first = 0
    for boxes, group, mine, then in (
        ((c1, c2, c3), x_pairs, x * NC + core, ((y_line, y), (z_line, z))),
        ((a1, a2, a3), y_pairs, y * NC + core, ((z_line, z), (x_line, x))),
        ((b1, b2, b3), z_pairs, z * NC + core, ((y_line, y), (x_line, x))),
    ):
        plan.append((first, boxes, group, mine, then))
        first += boxes[0].shape[0] * boxes[0].shape[1]

    def whole_of(box, peers):
        return box.at[pl.ds(0, len(peers))]

    for n, (first, boxes, group, mine, then) in enumerate(plan):
        size = boxes[0].shape[1]
        start(4 * n, group, lambda j: src.at[piece(first, size, j)], lambda j: boxes[0].at[j], mine)
        boxes[0][mine] = src[piece(first, size, mine), :]
    put_qpre.start()
    for hop in range(2):
        for n, (first, boxes, group, mine, then) in enumerate(plan):
            peers, here = then[hop]
            came = group if hop == 0 else then[0][0]
            bulk(4 * n + hop, came, whole_of(boxes[hop], came)).wait_recv()
            box = boxes[hop + 1]
            box[here] = added(boxes[hop])
            start(4 * n + 1 + hop, peers, lambda j: box.at[here], lambda j: box.at[j], here)
    for n, (first, boxes, group, mine, then) in enumerate(plan):
        size = boxes[0].shape[1]
        bulk(4 * n + 2, then[1][0], whole_of(boxes[2], then[1][0])).wait_recv()
        gathered[piece(first, size, mine), :] = added(boxes[2])
        start(
            4 * n + 3, group, lambda j: gathered.at[piece(first, size, mine)],
            lambda j: gathered.at[piece(first, size, j)], mine)
    for n, (first, boxes, group, mine, then) in enumerate(plan):
        size = boxes[0].shape[1]
        whole = gathered.at[pl.ds(first, len(group) * size)]
        bulk(4 * n + 3, group, whole).wait_recv()
    total_out[...] = gathered[...]

    for n, (first, boxes, group, mine, then) in enumerate(plan):
        size = boxes[0].shape[1]
        bulk(4 * n, group, whole_of(boxes[0], group)).wait_send()
        for hop in range(2):
            bulk(4 * n + 1 + hop, then[hop][0], whole_of(boxes[hop + 1], then[hop][0])).wait_send()
        bulk(4 * n + 3, group, gathered.at[pl.ds(first, len(group) * size)]).wait_send()
    for b in (1, 2):
        send_query(b).wait_send()
        send_grad(b).wait_send()
    for n in range(4):
        send_lse(n).wait_send()
    put_ppre.wait()
    put_qpre.wait()


def run_step(query_lengths, passage_lengths, positives, query_hidden, passage_hidden, projection):
    dma = pltpu.SemaphoreType.DMA
    smem = pl.BlockSpec(memory_space=pltpu.SMEM)
    vmem = pl.BlockSpec(memory_space=pltpu.VMEM)
    hbm = pl.BlockSpec(memory_space=pl.ANY)
    vm = pltpu.VMEM
    ny = NYH * NYL
    share = HID // 3
    ya, za, xa = ny * NC, NZ * NC, NX * NC
    return pl.pallas_call(
        step_kernel,
        out_shape=(
            jax.ShapeDtypeStruct((1, QR), F32),
            jax.ShapeDtypeStruct((PR, DIM), BF16),
            jax.ShapeDtypeStruct((DIM, QR), BF16),
            jax.ShapeDtypeStruct((HID, DIM), BF16),
        ),
        in_specs=[smem, smem, smem, hbm, hbm, hbm],
        out_specs=(vmem, hbm, hbm, vmem),
        scratch_shapes=[
            vm((QR, HID), BF16), vm((PR, HID), BF16), vm((HID, DIM), BF16),
            vm((3, QR, QR), BF16), vm((DIM, QR), F32), vm((1, QR), F32),
            vm((PR, 2 * DIM), BF16), vm((DIM, PR), BF16), vm((PR, DIM), F32), vm((PR, 1), F32),
            vm((3, PR, QR), F32), vm((3, PR, QR), BF16),
            vm((3, TAIL, QR), F32), vm((3, TAIL, QR), F32), vm((3, TAIL, QR), F32),
            vm((3, TAIL, QR), F32), vm((TAIL, QR), F32), vm((QR, QR), BF16),
            vm((8, QR), F32), vm((4, 8, QR), F32),
            vm((2, DIM, QR), BF16), vm((2, DIM, QR), BF16), vm((2, DIM, QR), BF16),
            vm((PR, DIM), BF16), vm((DIM, PR), BF16), vm((DIM, QR), BF16), vm((DIM, HID), F32),
            vm((HID, DIM), BF16),
            vm((ya, share // ya, DIM), BF16), vm((NZ, share // ya, DIM), BF16), vm((NX, share // ya, DIM), BF16),
            vm((za, share // za, DIM), BF16), vm((ny, share // za, DIM), BF16), vm((NX, share // za, DIM), BF16),
            vm((xa, share // xa, DIM), BF16), vm((ny, share // xa, DIM), BF16), vm((NZ, share // xa, DIM), BF16),
            vm((HID, DIM), BF16),
            dma((3,)), dma((2,)), dma((2,)), dma((2,)), dma((4,)), dma((4,)), dma((2,)), dma((2,)),
            dma((12,)), dma((12,)),
        ],
        compiler_params=pltpu.CompilerParams(collective_id=0, has_side_effects=True),
    )(query_lengths, passage_lengths, positives, query_hidden, passage_hidden, projection)


def finish_kernel(loss, ppre, qpre, proj, total, loss_out, gq_any, gp_any, gproj, held, sem):
    for q in range(QN):
        loss_out[q] = loss[0, q * QT]
    copies = []
    for t in range(HID // QR):
        columns = pl.ds(t * QR, QR)
        for h in range(2):
            spot = pl.ds(h * (PR // 2), PR // 2)
            held[spot, columns] = nt_dot(ppre[spot, :], proj[columns, :]).astype(BF16)
            copies.append(pltpu.make_async_copy(
                held.at[spot, columns], gp_any.at[spot, columns], sem.at[len(copies)]))
            copies[-1].start()
        if t == 0:
            spot = pl.ds(PR, QR)
            pre = qpre[...].astype(F32).T.astype(BF16)
            held[spot, :] = nt_dot(pre, proj[...]).astype(BF16)
            copies.append(pltpu.make_async_copy(held.at[spot], gq_any, sem.at[len(copies)]))
            copies[-1].start()
            for n in range(HID // DIM):
                spot = pl.ds(n * DIM, DIM)
                gproj[spot, :] = total[spot, :].astype(F32).T * (1.0 / (NB * NMP))
    for copy in copies:
        copy.wait()


def run_finish(loss, ppre, qpre, projection, total):
    smem = pl.BlockSpec(memory_space=pltpu.SMEM)
    vmem = pl.BlockSpec(memory_space=pltpu.VMEM)
    hbm = pl.BlockSpec(memory_space=pl.ANY)
    return pl.pallas_call(
        finish_kernel,
        out_shape=(
            jax.ShapeDtypeStruct((QN,), F32),
            jax.ShapeDtypeStruct((QR, HID), BF16),
            jax.ShapeDtypeStruct((PR, HID), BF16),
            jax.ShapeDtypeStruct((HID, DIM), F32),
        ),
        in_specs=[smem, vmem, vmem, vmem, vmem],
        out_specs=(smem, hbm, hbm, vmem),
        scratch_shapes=[
            pltpu.VMEM((PR + QR, HID), BF16),
            pltpu.SemaphoreType.DMA((2 * (HID // QR) + 1,)),
        ],
    )(loss, ppre, qpre, projection, total)


def per_device(query_hidden, passage_hidden, projection, query_lengths, passage_lengths, positives):
    loss, ppre, qpre, total = run_step(
        query_lengths, passage_lengths, positives, query_hidden, passage_hidden, projection)
    return run_finish(loss, ppre, qpre, projection, total)


def solution(mesh):
    in_specs = (
        P(("batch", "mp"), None),
        P(("batch", "mp"), None),
        P(),
        P(("batch", "mp")),
        P(("batch", "mp")),
        P(("batch", "mp")),
    )
    out_specs = (P(("batch", "mp")), P(("batch", "mp"), None), P(("batch", "mp"), None), P())
    return jax.shard_map(
        per_device, mesh=mesh, in_specs=in_specs, out_specs=out_specs, check_vma=False
    )
```

time: 65.4 us -> 61.3 us (0.937)
  Pallas kernels: 64.5 us -> 60.5 us
    pallas_call x1, Pallas kernels: 60.9 us -> 56.8 us  [run_step(): pl.pallas_call(step_kernel, out_shape=(jax.ShapeDtypeStruct((1, QR), F32)...]
where the time goes in v3:
time: 61.3 us; the launch traced here: 61.1 us
  Pallas kernels  60.5 us (99%)
  between operations  0.64 us (1%)
    pallas_call x1, Pallas kernels, run_step(): pl.pallas_call(step_kernel, out_shape=(jax.ShapeDtypeStruct((1, QR), F32)...  56.8 us
    pallas_call x1, Pallas kernels, run_finish(): pl.pallas_call(finish_kernel, out_shape=(jax.ShapeDtypeStruct((QN,), F32)...  3.68 us

profile of v3, /device:TPU:1, one launch (start us, length us, event | category | flops | bytes accessed | tf_op | source)
XLA Modules:
  0.0 61.1 jit_solution(5178846931936613031)
XLA Ops:
  0.6 56.8 %shard_map.93 = (f32[1,256]{1,0:T(1,128)}, bf16[1280,128]{1,0:T(8,128)(2,1)}, bf16[128,256]{1,0:T(8,128)(2,1)}, bf16[768,128]{1,0:T(8,128)(2,1)}) custom-call(s32[8]{0:T(128)} %qlen.1, s32[10]{0:T(128)} %plen.1, s32[8]{0:T(128)} %pos.1, bf16[256,768]{1,0:T(8,128)(2,1)} %qh_any.1, bf16[1280,768]{1,0:T(8,128)(2,1)} %ph_any.1, bf16[768,128]{1,0:T(8,128)(2,1)} %proj.1), custom_call_target="tpu_custom_call" | custom-call | tf_op jit(solution)/shard_map/pallas_call | solution.py:356
  57.5 3.7 %shard_map.94 = (f32[8]{0:T(128)}, bf16[256,768]{1,0:T(8,128)(2,1)}, bf16[1280,768]{1,0:T(8,128)(2,1)}, f32[768,128]{1,0:T(8,128)}) custom-call(f32[1,256]{1,0:T(1,128)} %get-tuple-element.8.loss, bf16[1280,128]{1,0:T(8,128)(2,1)} %get-tuple-element.9.ppre, bf16[128,256]{1,0:T(8,128)(2,1)} %get-tuple-element.10.qpre, bf16[768,128]{1,0:T(8,128)(2,1)} %proj.1, ...), custom_call_target="tpu_custom_call" | custom-call | tf_op jit(solution)/shard_map/pallas_call | solution.py:417

commit v4 on v3

--- a/solution.py
+++ b/solution.py
@@ -48,12 +48,12 @@
 
 
 def step_kernel(
-    qlen, plen, pos, qh_any, ph_any, proj_any,
-    loss_out, ppre_any, qpre_any, total_out,
-    qh, ph, proj, qbuf, qunit, qrad, paug, ptr, punit, prad, power, gsim,
+    qlen_any, plen_any, pos_any, qh_any, ph_any, proj_any,
+    loss_out, hidden_out_ref, total_out,
+    qlen, plen, pos, both, proj, qbuf, qunit, qrad, paug, ptr, punit, prad, power, gsim,
     tops, tots, score, keeps, coef, member, lse_own, lse_in, tq_out, tq_in, qscaled,
-    ppre, ppre_t, qpre, ppart, src, a1, a2, a3, b1, b2, b3, c1, c2, c3, gathered,
-    in_sem, out_sem, qs, qr, ls, lr, ts, tr, push, pull,
+    ppre, pre_t, src, a1, a2, a3, a4, b1, b2, b3, b4, c1, c2, c3, c4, gathered,
+    in_sem, qs, qr, ls, lr, ts, tr, push, pull,
 ):
     bi = lax.axis_index("batch")
     mi = lax.axis_index("mp")
@@ -65,26 +65,18 @@
     core = lax.rem(mi, NC)
     y = yh * NYL + yl
     xz = bi - yh
-    cores = turned(core, NC)
-
-    def at_y(spot, side):
-        return (xz + lax.div(spot, NYL), lax.rem(spot, NYL) * NC + side)
-
-    def at_z(spot, side):
-        return (bi + (spot - z) * NYH, mi + (side - core))
-
-    def at_x(spot, side):
-        return (bi + (spot - x) * (NYH * NZ), mi + (side - core))
-
-    def pairs(spots, place):
-        return [(spot * NC + side, place(spot, side)) for a, spot in spots for c, side in cores if a or c]
-
-    def lines(spots, place):
-        return [(spot, place(spot, core)) for a, spot in spots if a]
-
-    ys, zs, xs = turned(y, NYH * NYL), turned(z, NZ), turned(x, NX)
-    y_pairs, z_pairs, x_pairs = pairs(ys, at_y), pairs(zs, at_z), pairs(xs, at_x)
-    y_line, z_line, x_line = lines(ys, at_y), lines(zs, at_z), lines(xs, at_x)
+
+    def at_y(spot):
+        return (xz + lax.div(spot, NYL), lax.rem(spot, NYL) * NC + core)
+
+    def at_z(spot):
+        return (bi + (spot - z) * NYH, mi)
+
+    def at_x(spot):
+        return (bi + (spot - x) * (NYH * NZ), mi)
+
+    def line(here, count, place):
+        return [(spot, place(spot)) for a, spot in turned(here, count) if a]
 
     def ring_peer(hop):
         there = bi + hop
@@ -93,18 +85,39 @@
 
     ring = {hop: ring_peer(hop) for hop in HOPS}
 
+    whole_p, whole_q = pl.ds(0, PR), pl.ds(PR, QR)
     get_proj = pltpu.make_async_copy(proj_any, proj, in_sem.at[0])
-    get_qh = pltpu.make_async_copy(qh_any, qh, in_sem.at[1])
-    get_ph = pltpu.make_async_copy(ph_any, ph, in_sem.at[2])
-    get_proj.start()
-    get_qh.start()
-    get_ph.start()
+    get_qh = pltpu.make_async_copy(qh_any, both.at[whole_q], in_sem.at[1])
+    get_ph = pltpu.make_async_copy(ph_any, both.at[whole_p], in_sem.at[2])
+
+    small = [
+        pltpu.make_async_copy(far, near, in_sem.at[3 + n])
+        for n, (far, near) in enumerate(((qlen_any, qlen), (plen_any, plen), (pos_any, pos)))]
+
+    @pl.when(bi >= 0)
+    def _():
+        for copy in small:
+            copy.start()
+        get_proj.start()
+        get_qh.start()
+        get_ph.start()
 
     barrier = pltpu.get_barrier_semaphore()
-    everyone = [ring[hop] for hop in HOPS] + [w for _, w in y_pairs + z_pairs + x_pairs]
-    for where in everyone:
-        pl.semaphore_signal(barrier, inc=1, device_id=where, device_id_type=MESH)
-
+
+    def greet(places):
+        for where in places:
+            pl.semaphore_signal(barrier, inc=1, device_id=where, device_id_type=MESH)
+        return len(places)
+
+    greeted = greet([ring[hop] for hop in HOPS])
+    y_line = line(y, NYH * NYL, at_y)
+    z_line = line(z, NZ, at_z)
+    x_line = line(x, NX, at_x)
+    partner = [(NC - 1 - core, (bi, mi + (NC - 1 - 2 * core)))]
+    greeted += greet([where for _, where in y_line + z_line + x_line + partner])
+
+    for copy in small:
+        copy.wait()
     lane = exact_iota((1, QR), 1)
     keep = jnp.zeros((1, QR), F32)
     for q in range(QN):
@@ -118,7 +131,7 @@
 
     get_proj.wait()
     get_qh.wait()
-    before = jnp.dot(qh[...], proj[...], preferred_element_type=F32).T
+    before = jnp.dot(both[whole_q, :], proj[...], preferred_element_type=F32).T
     radius = jnp.sqrt(jnp.sum(before * before, axis=0, keepdims=True) + norm_eps)
     inverse = 1.0 / radius
     unit = before * inverse
@@ -126,7 +139,7 @@
     qrad[...] = inverse
     qbuf[0, :DIM, :] = unit.astype(BF16)
 
-    pl.semaphore_wait(barrier, len(everyone))
+    pl.semaphore_wait(barrier, greeted)
 
     def send_query(b):
         part = pl.ds(0, DIM + TAIL)
@@ -152,7 +165,7 @@
 
     for r in range(PR // CHUNK):
         spot = pl.ds(r * CHUNK, CHUNK)
-        before = jnp.dot(ph[spot, :], proj[...], preferred_element_type=F32)
+        before = jnp.dot(both[spot, :], proj[...], preferred_element_type=F32)
         radius = jnp.sqrt(jnp.sum(before * before, axis=-1, keepdims=True) + norm_eps)
         inverse = 1.0 / radius
         unit = before * inverse
@@ -253,13 +266,9 @@
         pre = (grad - unit * jnp.sum(unit * grad, axis=-1, keepdims=True)) * prad[spot, :]
         pre = pre.astype(BF16)
         ppre[spot, :] = pre
-        ppre_t[:, spot] = pre.astype(F32).T.astype(BF16)
-
-    put_ppre = pltpu.make_async_copy(ppre, ppre_any, out_sem.at[0])
-    put_ppre.start()
-    ppart[...] = jnp.dot(ppre_t[...], ph[...], preferred_element_type=F32)
+        pre_t[:, spot] = pre.astype(F32).T.astype(BF16)
+
     qgrad = jnp.dot(ptr[...], gsim[0], preferred_element_type=F32)
-
     send_grad(1).wait_recv()
     send_grad(2).wait_recv()
     qgrad += jnp.exp(lse_in[2, 1:2, :] - totals[0]) * tq_in[0].astype(F32)
@@ -267,11 +276,7 @@
     unit = qunit[...]
     pre = (qgrad - unit * jnp.sum(unit * qgrad, axis=0, keepdims=True)) * qrad[...]
     pre = pre.astype(BF16)
-    qpre[...] = pre
-    part = ppart[...] + jnp.dot(pre, qh[...], preferred_element_type=F32)
-    for t in range(HID // DIM):
-        src[t * DIM:(t + 1) * DIM, :] = part[:, t * DIM:(t + 1) * DIM].astype(BF16)
-    put_qpre = pltpu.make_async_copy(qpre, qpre_any, out_sem.at[1])
+    pre_t[:, whole_q] = pre
 
     def piece(first, size, j):
         return pl.ds(pl.multiple_of(first + j * size, size), size)
@@ -290,81 +295,91 @@
     def added(box):
         return jnp.sum(box[...].astype(F32), axis=0).astype(BF16)
 
-    plan = []
-    first = 0
-    for boxes, group, mine, then in (
-        ((c1, c2, c3), x_pairs, x * NC + core, ((y_line, y), (z_line, z))),
-        ((a1, a2, a3), y_pairs, y * NC + core, ((z_line, z), (x_line, x))),
-        ((b1, b2, b3), z_pairs, z * NC + core, ((y_line, y), (x_line, x))),
-    ):
-        plan.append((first, boxes, group, mine, then))
-        first += boxes[0].shape[0] * boxes[0].shape[1]
-
-    def whole_of(box, peers):
-        return box.at[pl.ds(0, len(peers))]
-
-    for n, (first, boxes, group, mine, then) in enumerate(plan):
+    along_y, along_z, along_x, across = (y_line, y), (z_line, z), (x_line, x), (partner, core)
+    plan = (
+        ((a1, a2, a3, a4), (along_y, along_z, along_x, across)),
+        ((b1, b2, b3, b4), (along_z, along_y, along_x, across)),
+        ((c1, c2, c3, c4), (along_x, along_y, along_z, across)),
+    )
+    share = HID // 3
+    def arrived(n, hop):
+        boxes, route = plan[n]
+        peers = route[hop][0]
+        bulk(5 * n + hop, peers, boxes[hop].at[pl.ds(0, len(peers))]).wait_recv()
+
+    for n, (boxes, route) in enumerate(plan):
+        peers, mine = route[0]
         size = boxes[0].shape[1]
-        start(4 * n, group, lambda j: src.at[piece(first, size, j)], lambda j: boxes[0].at[j], mine)
-        boxes[0][mine] = src[piece(first, size, mine), :]
-    put_qpre.start()
-    for hop in range(2):
-        for n, (first, boxes, group, mine, then) in enumerate(plan):
-            peers, here = then[hop]
-            came = group if hop == 0 else then[0][0]
-            bulk(4 * n + hop, came, whole_of(boxes[hop], came)).wait_recv()
+        part = jnp.dot(pre_t[...], both[:, n * share:(n + 1) * share], preferred_element_type=F32)
+        for t in range(share // DIM):
+            src[n * share + t * DIM:n * share + (t + 1) * DIM, :] = (
+                part[:, t * DIM:(t + 1) * DIM].astype(BF16))
+        start(5 * n, peers, lambda j: src.at[piece(n * share, size, j)], lambda j: boxes[0].at[j], mine)
+        boxes[0][mine] = src[piece(n * share, size, mine), :]
+
+    def hidden_tile(r):
+        spot = pl.ds(r * CHUNK, CHUNK)
+        rows = pre_t[:, whole_q].astype(F32).T.astype(BF16) if r == PR // CHUNK else ppre[spot, :]
+        hidden_out_ref[spot, :] = nt_dot(rows, proj[...]).astype(BF16)
+
+    for hop in range(3):
+        for r in (2 * hop, 2 * hop + 1):
+            hidden_tile(r)
+        for n, (boxes, route) in enumerate(plan):
+            peers, here = route[hop + 1]
             box = boxes[hop + 1]
+            arrived(n, hop)
             box[here] = added(boxes[hop])
-            start(4 * n + 1 + hop, peers, lambda j: box.at[here], lambda j: box.at[j], here)
-    for n, (first, boxes, group, mine, then) in enumerate(plan):
+            start(5 * n + hop + 1, peers, lambda j: box.at[here], lambda j: box.at[j], here)
+    for n, (boxes, route) in enumerate(plan):
+        peers, mine = route[0]
         size = boxes[0].shape[1]
-        bulk(4 * n + 2, then[1][0], whole_of(boxes[2], then[1][0])).wait_recv()
-        gathered[piece(first, size, mine), :] = added(boxes[2])
+        arrived(n, 3)
+        gathered[piece(n * share, size, mine), :] = added(boxes[3])
         start(
-            4 * n + 3, group, lambda j: gathered.at[piece(first, size, mine)],
-            lambda j: gathered.at[piece(first, size, j)], mine)
-    for n, (first, boxes, group, mine, then) in enumerate(plan):
-        size = boxes[0].shape[1]
-        whole = gathered.at[pl.ds(first, len(group) * size)]
-        bulk(4 * n + 3, group, whole).wait_recv()
+            5 * n + 4, peers, lambda j: gathered.at[piece(n * share, size, mine)],
+            lambda j: gathered.at[piece(n * share, size, j)], mine)
+
+    def spread(n):
+        boxes, route = plan[n]
+        peers = route[0][0]
+        return bulk(5 * n + 4, peers, gathered.at[pl.ds(n * share, len(peers) * boxes[0].shape[1])])
+
+    for n in range(3):
+        spread(n).wait_recv()
     total_out[...] = gathered[...]
 
-    for n, (first, boxes, group, mine, then) in enumerate(plan):
-        size = boxes[0].shape[1]
-        bulk(4 * n, group, whole_of(boxes[0], group)).wait_send()
-        for hop in range(2):
-            bulk(4 * n + 1 + hop, then[hop][0], whole_of(boxes[hop + 1], then[hop][0])).wait_send()
-        bulk(4 * n + 3, group, gathered.at[pl.ds(first, len(group) * size)]).wait_send()
+    for n, (boxes, route) in enumerate(plan):
+        for hop in range(4):
+            peers = route[hop][0]
+            bulk(5 * n + hop, peers, boxes[hop].at[pl.ds(0, len(peers))]).wait_send()
+        spread(n).wait_send()
     for b in (1, 2):
         send_query(b).wait_send()
         send_grad(b).wait_send()
     for n in range(4):
         send_lse(n).wait_send()
-    put_ppre.wait()
-    put_qpre.wait()
 
 
 def run_step(query_lengths, passage_lengths, positives, query_hidden, passage_hidden, projection):
     dma = pltpu.SemaphoreType.DMA
-    smem = pl.BlockSpec(memory_space=pltpu.SMEM)
     vmem = pl.BlockSpec(memory_space=pltpu.VMEM)
-    hbm = pl.BlockSpec(memory_space=pl.ANY)
+    hbm = pl.BlockSpec(memory_space=pltpu.HBM)
     vm = pltpu.VMEM
     ny = NYH * NYL
     share = HID // 3
-    ya, za, xa = ny * NC, NZ * NC, NX * NC
     return pl.pallas_call(
         step_kernel,
         out_shape=(
             jax.ShapeDtypeStruct((1, QR), F32),
-            jax.ShapeDtypeStruct((PR, DIM), BF16),
-            jax.ShapeDtypeStruct((DIM, QR), BF16),
+            jax.ShapeDtypeStruct((PR + QR, HID), BF16),
             jax.ShapeDtypeStruct((HID, DIM), BF16),
         ),
-        in_specs=[smem, smem, smem, hbm, hbm, hbm],
-        out_specs=(vmem, hbm, hbm, vmem),
+        in_specs=[hbm] * 6,
+        out_specs=(vmem, vmem, vmem),
         scratch_shapes=[
-            vm((QR, HID), BF16), vm((PR, HID), BF16), vm((HID, DIM), BF16),
+            pltpu.SMEM((QN,), jnp.int32), pltpu.SMEM((PN,), jnp.int32), pltpu.SMEM((QN,), jnp.int32),
+            vm((PR + QR, HID), BF16), vm((HID, DIM), BF16),
             vm((3, QR, QR), BF16), vm((DIM, QR), F32), vm((1, QR), F32),
             vm((PR, 2 * DIM), BF16), vm((DIM, PR), BF16), vm((PR, DIM), F32), vm((PR, 1), F32),
             vm((3, PR, QR), F32), vm((3, PR, QR), BF16),
@@ -372,45 +387,38 @@
             vm((3, TAIL, QR), F32), vm((TAIL, QR), F32), vm((QR, QR), BF16),
             vm((8, QR), F32), vm((4, 8, QR), F32),
             vm((2, DIM, QR), BF16), vm((2, DIM, QR), BF16), vm((2, DIM, QR), BF16),
-            vm((PR, DIM), BF16), vm((DIM, PR), BF16), vm((DIM, QR), BF16), vm((DIM, HID), F32),
+            vm((PR, DIM), BF16), vm((DIM, PR + QR), BF16),
             vm((HID, DIM), BF16),
-            vm((ya, share // ya, DIM), BF16), vm((NZ, share // ya, DIM), BF16), vm((NX, share // ya, DIM), BF16),
-            vm((za, share // za, DIM), BF16), vm((ny, share // za, DIM), BF16), vm((NX, share // za, DIM), BF16),
-            vm((xa, share // xa, DIM), BF16), vm((ny, share // xa, DIM), BF16), vm((NZ, share // xa, DIM), BF16),
+            vm((ny, share // ny, DIM), BF16), vm((NZ, share // ny, DIM), BF16),
+            vm((NX, share // ny, DIM), BF16), vm((NC, share // ny, DIM), BF16),
+            vm((NZ, share // NZ, DIM), BF16), vm((ny, share // NZ, DIM), BF16),
+            vm((NX, share // NZ, DIM), BF16), vm((NC, share // NZ, DIM), BF16),
+            vm((NX, share // NX, DIM), BF16), vm((ny, share // NX, DIM), BF16),
+            vm((NZ, share // NX, DIM), BF16), vm((NC, share // NX, DIM), BF16),
             vm((HID, DIM), BF16),
-            dma((3,)), dma((2,)), dma((2,)), dma((2,)), dma((4,)), dma((4,)), dma((2,)), dma((2,)),
-            dma((12,)), dma((12,)),
+            dma((6,)), dma((2,)), dma((2,)), dma((4,)), dma((4,)), dma((2,)), dma((2,)),
+            dma((15,)), dma((15,)),
         ],
-        compiler_params=pltpu.CompilerParams(collective_id=0, has_side_effects=True),
+        compiler_params=pltpu.CompilerParams(
+            collective_id=0, has_side_effects=True, vmem_limit_bytes=24 * 1024 * 1024),
     )(query_lengths, passage_lengths, positives, query_hidden, passage_hidden, projection)
 
 
-def finish_kernel(loss, ppre, qpre, proj, total, loss_out, gq_any, gp_any, gproj, held, sem):
+def finish_kernel(loss, hidden, total, loss_out, gq_any, gp_any, gproj, sem):
+    put_p = pltpu.make_async_copy(hidden.at[pl.ds(0, PR)], gp_any, sem.at[0])
+    put_q = pltpu.make_async_copy(hidden.at[pl.ds(PR, QR)], gq_any, sem.at[1])
+    put_p.start()
+    put_q.start()
     for q in range(QN):
         loss_out[q] = loss[0, q * QT]
-    copies = []
-    for t in range(HID // QR):
-        columns = pl.ds(t * QR, QR)
-        for h in range(2):
-            spot = pl.ds(h * (PR // 2), PR // 2)
-            held[spot, columns] = nt_dot(ppre[spot, :], proj[columns, :]).astype(BF16)
-            copies.append(pltpu.make_async_copy(
-                held.at[spot, columns], gp_any.at[spot, columns], sem.at[len(copies)]))
-            copies[-1].start()
-        if t == 0:
-            spot = pl.ds(PR, QR)
-            pre = qpre[...].astype(F32).T.astype(BF16)
-            held[spot, :] = nt_dot(pre, proj[...]).astype(BF16)
-            copies.append(pltpu.make_async_copy(held.at[spot], gq_any, sem.at[len(copies)]))
-            copies[-1].start()
-            for n in range(HID // DIM):
-                spot = pl.ds(n * DIM, DIM)
-                gproj[spot, :] = total[spot, :].astype(F32).T * (1.0 / (NB * NMP))
-    for copy in copies:
-        copy.wait()
-
-
-def run_finish(loss, ppre, qpre, projection, total):
+    for n in range(HID // DIM):
+        spot = pl.ds(n * DIM, DIM)
+        gproj[spot, :] = total[spot, :].astype(F32).T * (1.0 / (NB * NMP))
+    put_p.wait()
+    put_q.wait()
+
+
+def run_finish(loss, hidden, total):
     smem = pl.BlockSpec(memory_space=pltpu.SMEM)
     vmem = pl.BlockSpec(memory_space=pltpu.VMEM)
     hbm = pl.BlockSpec(memory_space=pl.ANY)
@@ -422,19 +430,18 @@
             jax.ShapeDtypeStruct((PR, HID), BF16),
             jax.ShapeDtypeStruct((HID, DIM), F32),
         ),
-        in_specs=[smem, vmem, vmem, vmem, vmem],
+        in_specs=[smem, vmem, vmem],
         out_specs=(smem, hbm, hbm, vmem),
-        scratch_shapes=[
-            pltpu.VMEM((PR + QR, HID), BF16),
-            pltpu.SemaphoreType.DMA((2 * (HID // QR) + 1,)),
-        ],
-    )(loss, ppre, qpre, projection, total)
+        scratch_shapes=[pltpu.SemaphoreType.DMA((2,))],
+        compiler_params=pltpu.CompilerParams(vmem_limit_bytes=16 * 1024 * 1024),
+    )(loss, hidden, total)
 
 
 def per_device(query_hidden, passage_hidden, projection, query_lengths, passage_lengths, positives):
-    loss, ppre, qpre, total = run_step(
-        query_lengths, passage_lengths, positives, query_hidden, passage_hidden, projection)
-    return run_finish(loss, ppre, qpre, projection, total)
+    loss, hidden, total = run_step(*(
+        pltpu.with_memory_space_constraint(v, pltpu.HBM) for v in (
+            query_lengths, passage_lengths, positives, query_hidden, passage_hidden, projection)))
+    return run_finish(loss, hidden, total)
 
 
 def solution(mesh):

time: 61.3 us -> 60.6 us (0.989)
  Pallas kernels: 60.5 us -> 59.8 us
    pallas_call x1, Pallas kernels: 3.68 us -> 2.75 us  [run_finish(): pl.pallas_call(finish_kernel, out_shape=(jax.ShapeDtypeStruct((QN,), F32)...]
where the time goes in v4:
time: 60.6 us; the launch traced here: 60.4 us
  Pallas kernels  59.8 us (99%)
  between operations  0.64 us (1%)
    pallas_call x1, Pallas kernels, run_step(): pl.pallas_call(step_kernel, out_shape=(jax.ShapeDtypeStruct((1, QR), F32)...  57 us
    pallas_call x1, Pallas kernels, run_finish(): pl.pallas_call(finish_kernel, out_shape=(jax.ShapeDtypeStruct((QN,), F32)...  2.75 us

profile of v4, /device:TPU:1, one launch (start us, length us, event | category | flops | bytes accessed | tf_op | source)
XLA Modules:
  0.0 60.4 jit_solution(7286795483644077529)
XLA Ops:
  0.6 57.0 %shard_map.93 = (f32[1,256]{1,0:T(1,128)S(1)}, bf16[1536,768]{1,0:T(8,128)(2,1)S(1)}, bf16[768,128]{1,0:T(8,128)(2,1)S(1)}) custom-call(s32[8]{0:T(128)} %qlen_any.1, s32[10]{0:T(128)} %plen_any.1, s32[8]{0:T(128)} %pos_any.1, bf16[256,768]{1,0:T(8,128)(2,1)} %qh_any.1, bf16[1280,768]{1,0:T(8,128)(2,1)} %ph_any.1, bf16[768,128]{1,0:T(8,128)(2,1)} %proj_any.1), custom_call_target="tpu_custom_call" | custom-call | tf_op jit(solution)/shard_map/pallas_call | solution.py:371
  57.7 2.7 %shard_map.94 = (f32[8]{0:T(128)}, bf16[256,768]{1,0:T(8,128)(2,1)}, bf16[1280,768]{1,0:T(8,128)(2,1)}, f32[768,128]{1,0:T(8,128)}) custom-call(f32[1,256]{1,0:T(1,128)S(1)} %get-tuple-element.7.loss, bf16[1536,768]{1,0:T(8,128)(2,1)S(1)} %get-tuple-element.8.hidden, bf16[768,128]{1,0:T(8,128)(2,1)S(1)} %get-tuple-element.9.total), custom_call_target="tpu_custom_call" | custom-call | tf_op jit(solution)/shard_map/pallas_call | solution.py:425

commit v5 on v4

--- a/solution.py
+++ b/solution.py
@@ -21,6 +21,7 @@
 QR, PR, DIM, HID = QN * QT, PN * PT, 128, 768
 TAIL = 16
 HOPS = (1, 2, -1, -2)
+LSE_READY = (1, 0, 2, 2)
 CHUNK = 256
 UNROLL = 2
 
@@ -52,7 +53,7 @@
     loss_out, hidden_out_ref, total_out,
     qlen, plen, pos, both, proj, qbuf, qunit, qrad, paug, ptr, punit, prad, power, gsim,
     tops, tots, score, keeps, coef, member, lse_own, lse_in, tq_out, tq_in, qscaled,
-    ppre, pre_t, src, a1, a2, a3, a4, b1, b2, b3, b4, c1, c2, c3, c4, gathered,
+    ppre, pre_t, pgrad, ppart, src, a1, a2, a3, a4, b1, b2, b3, b4, c1, c2, c3, c4, gathered,
     in_sem, qs, qr, ls, lr, ts, tr, push, pull,
 ):
     bi = lax.axis_index("batch")
@@ -204,8 +205,8 @@
         score[b] = scores
         top = jnp.max(scores, axis=0, keepdims=True)
         total = top + jnp.log(jnp.sum(jnp.exp(scores - top), axis=0, keepdims=True))
-        lse_own[pl.ds(b, 1), :] = total
-        return total
+        for k in range(b, 3):
+            lse_own[k, b:b + 1, :] = total
 
     def to_grads(b, dscore):
         coef[...] = dscore * keeps[b] * (outer_scale * loss_scale) / tots[b]
@@ -224,18 +225,19 @@
 
     def send_lse(n):
         return pltpu.make_async_remote_copy(
-            src_ref=lse_own, dst_ref=lse_in.at[n], send_sem=ls.at[n], recv_sem=lr.at[n],
+            src_ref=lse_own.at[LSE_READY[n]], dst_ref=lse_in.at[n], send_sem=ls.at[n], recv_sem=lr.at[n],
             device_id=ring[HOPS[n]], device_id_type=MESH)
 
     lse_own[...] = jnp.zeros(lse_own.shape, F32)
-    own = [forward(0)]
-    for b in (1, 2):
-        send_query(b).wait_recv()
-        own.append(forward(b))
-    for n in range(4):
-        send_lse(n).start()
+    for b in range(3):
+        if b:
+            send_query(b).wait_recv()
+        forward(b)
+        for n in range(4):
+            if LSE_READY[n] == b:
+                send_lse(n).start()
     for b in (2, 1):
-        to_grads(b, jnp.exp(score[b] - lse_own[b:b + 1, :]))
+        to_grads(b, jnp.exp(score[b] - lse_own[2, b:b + 1, :]))
         tq_out[b - 1] = jnp.dot(ptr[...], gsim[b], preferred_element_type=F32).astype(BF16)
         send_grad(b).start()
 
@@ -244,35 +246,37 @@
         place = jnp.where(lane // QT == q, pos[q], place)
     onehot = jnp.where(exact_iota((TAIL, QR), 0) == place, 1.0, 0.0)
 
-    for n in range(4):
-        send_lse(n).wait_recv()
-    totals = (
-        log_sum((lse_own[0:1, :], lse_in[2, 1:2, :], lse_in[3, 2:3, :])),
-        log_sum((lse_in[0, 0:1, :], lse_own[1:2, :], lse_in[2, 2:3, :])),
-        log_sum((lse_in[1, 0:1, :], lse_in[0, 1:2, :], lse_own[2:3, :])),
-    )
-    loss_out[...] = totals[0] - jnp.sum(onehot * score[0], axis=0, keepdims=True)
-    for b in (1, 2):
-        factor = jnp.exp(lse_own[b:b + 1, :] - totals[b])
+    def scaled(b, rows):
+        factor = jnp.exp(lse_own[2, b:b + 1, :] - log_sum(rows))
         qscaled[b - 1] = (qbuf[b, :DIM, :].astype(F32) * factor).astype(BF16)
-    to_grads(0, jnp.exp(score[0] - totals[0]) - onehot)
+
+    send_lse(0).wait_recv()
+    send_lse(1).wait_recv()
+    scaled(2, (lse_in[1, 0:1, :], lse_in[0, 1:2, :], lse_own[2, 2:3, :]))
+    pgrad[...] = nt_dot(gsim[2], qscaled[1])
+    send_lse(2).wait_recv()
+    scaled(1, (lse_in[0, 0:1, :], lse_own[2, 1:2, :], lse_in[2, 2:3, :]))
+    pgrad[...] += nt_dot(gsim[1], qscaled[0])
+    send_lse(3).wait_recv()
+    total = log_sum((lse_own[2, 0:1, :], lse_in[2, 1:2, :], lse_in[3, 2:3, :]))
+    to_grads(0, jnp.exp(score[0] - total) - onehot)
 
     for r in range(PR // CHUNK):
         spot = pl.ds(r * CHUNK, CHUNK)
-        grad = nt_dot(gsim[0, spot, :], qbuf[0, :DIM, :])
-        grad += nt_dot(gsim[1, spot, :], qscaled[0])
-        grad += nt_dot(gsim[2, spot, :], qscaled[1])
+        grad = pgrad[spot, :] + nt_dot(gsim[0, spot, :], qbuf[0, :DIM, :])
         unit = punit[spot, :]
         pre = (grad - unit * jnp.sum(unit * grad, axis=-1, keepdims=True)) * prad[spot, :]
         pre = pre.astype(BF16)
         ppre[spot, :] = pre
         pre_t[:, spot] = pre.astype(F32).T.astype(BF16)
 
+    ppart[...] = jnp.dot(pre_t[:, whole_p], both[whole_p, :], preferred_element_type=F32)
     qgrad = jnp.dot(ptr[...], gsim[0], preferred_element_type=F32)
+
     send_grad(1).wait_recv()
     send_grad(2).wait_recv()
-    qgrad += jnp.exp(lse_in[2, 1:2, :] - totals[0]) * tq_in[0].astype(F32)
-    qgrad += jnp.exp(lse_in[3, 2:3, :] - totals[0]) * tq_in[1].astype(F32)
+    qgrad += jnp.exp(lse_in[2, 1:2, :] - total) * tq_in[0].astype(F32)
+    qgrad += jnp.exp(lse_in[3, 2:3, :] - total) * tq_in[1].astype(F32)
     unit = qunit[...]
     pre = (qgrad - unit * jnp.sum(unit * qgrad, axis=0, keepdims=True)) * qrad[...]
     pre = pre.astype(BF16)
@@ -310,7 +314,8 @@
     for n, (boxes, route) in enumerate(plan):
         peers, mine = route[0]
         size = boxes[0].shape[1]
-        part = jnp.dot(pre_t[...], both[:, n * share:(n + 1) * share], preferred_element_type=F32)
+        columns = pl.ds(n * share, share)
+        part = ppart[:, columns] + jnp.dot(pre, both[whole_q, columns], preferred_element_type=F32)
         for t in range(share // DIM):
             src[n * share + t * DIM:n * share + (t + 1) * DIM, :] = (
                 part[:, t * DIM:(t + 1) * DIM].astype(BF16))
@@ -322,16 +327,16 @@
         rows = pre_t[:, whole_q].astype(F32).T.astype(BF16) if r == PR // CHUNK else ppre[spot, :]
         hidden_out_ref[spot, :] = nt_dot(rows, proj[...]).astype(BF16)
 
-    for hop in range(3):
-        for r in (2 * hop, 2 * hop + 1):
-            hidden_tile(r)
-        for n, (boxes, route) in enumerate(plan):
-            peers, here = route[hop + 1]
-            box = boxes[hop + 1]
-            arrived(n, hop)
-            box[here] = added(boxes[hop])
-            start(5 * n + hop + 1, peers, lambda j: box.at[here], lambda j: box.at[j], here)
-    for n, (boxes, route) in enumerate(plan):
+    def onward(n, hop):
+        boxes, route = plan[n]
+        peers, here = route[hop + 1]
+        box = boxes[hop + 1]
+        arrived(n, hop)
+        box[here] = added(boxes[hop])
+        start(5 * n + hop + 1, peers, lambda j: box.at[here], lambda j: box.at[j], here)
+
+    def share_out(n):
+        boxes, route = plan[n]
         peers, mine = route[0]
         size = boxes[0].shape[1]
         arrived(n, 3)
@@ -339,6 +344,26 @@
         start(
             5 * n + 4, peers, lambda j: gathered.at[piece(n * share, size, mine)],
             lambda j: gathered.at[piece(n * share, size, j)], mine)
+
+    loss = total - jnp.sum(onehot * score[0], axis=0, keepdims=True)
+    for q in range(QN):
+        loss_out[q] = jnp.sum(jnp.where(lane == q * QT, loss, 0.0))
+    hidden_tile(0)
+    hidden_tile(1)
+    for n in range(3):
+        onward(n, 0)
+    hidden_tile(2)
+    hidden_tile(3)
+    for n in (2, 0, 1):
+        onward(n, 1)
+    hidden_tile(4)
+    hidden_tile(5)
+    for n in (0, 1):
+        onward(n, 2)
+    for n in (0, 1):
+        share_out(n)
+    onward(2, 2)
+    share_out(2)
 
     def spread(n):
         boxes, route = plan[n]
@@ -371,12 +396,12 @@
     return pl.pallas_call(
         step_kernel,
         out_shape=(
-            jax.ShapeDtypeStruct((1, QR), F32),
+            jax.ShapeDtypeStruct((QN,), F32),
             jax.ShapeDtypeStruct((PR + QR, HID), BF16),
             jax.ShapeDtypeStruct((HID, DIM), BF16),
         ),
         in_specs=[hbm] * 6,
-        out_specs=(vmem, vmem, vmem),
+        out_specs=(pl.BlockSpec(memory_space=pltpu.SMEM), vmem, vmem),
         scratch_shapes=[
             pltpu.SMEM((QN,), jnp.int32), pltpu.SMEM((PN,), jnp.int32), pltpu.SMEM((QN,), jnp.int32),
             vm((PR + QR, HID), BF16), vm((HID, DIM), BF16),
@@ -385,9 +410,10 @@
             vm((3, PR, QR), F32), vm((3, PR, QR), BF16),
             vm((3, TAIL, QR), F32), vm((3, TAIL, QR), F32), vm((3, TAIL, QR), F32),
             vm((3, TAIL, QR), F32), vm((TAIL, QR), F32), vm((QR, QR), BF16),
-            vm((8, QR), F32), vm((4, 8, QR), F32),
+            vm((3, 8, QR), F32), vm((4, 8, QR), F32),
             vm((2, DIM, QR), BF16), vm((2, DIM, QR), BF16), vm((2, DIM, QR), BF16),
             vm((PR, DIM), BF16), vm((DIM, PR + QR), BF16),
+            vm((PR, DIM), F32), vm((DIM, HID), F32),
             vm((HID, DIM), BF16),
             vm((ny, share // ny, DIM), BF16), vm((NZ, share // ny, DIM), BF16),
             vm((NX, share // ny, DIM), BF16), vm((NC, share // ny, DIM), BF16),
@@ -404,22 +430,23 @@
     )(query_lengths, passage_lengths, positives, query_hidden, passage_hidden, projection)
 
 
-def finish_kernel(loss, hidden, total, loss_out, gq_any, gp_any, gproj, sem):
-    put_p = pltpu.make_async_copy(hidden.at[pl.ds(0, PR)], gp_any, sem.at[0])
-    put_q = pltpu.make_async_copy(hidden.at[pl.ds(PR, QR)], gq_any, sem.at[1])
-    put_p.start()
-    put_q.start()
-    for q in range(QN):
-        loss_out[q] = loss[0, q * QT]
+def finish_kernel(loss, hidden, total, loss_any, gq_any, gp_any, gproj_any, gproj, sem):
+    puts = [
+        pltpu.make_async_copy(near, far, sem.at[n])
+        for n, (near, far) in enumerate((
+            (hidden.at[pl.ds(0, PR)], gp_any), (hidden.at[pl.ds(PR, QR)], gq_any),
+            (loss, loss_any), (gproj, gproj_any)))]
+    for put in puts[:3]:
+        put.start()
     for n in range(HID // DIM):
         spot = pl.ds(n * DIM, DIM)
         gproj[spot, :] = total[spot, :].astype(F32).T * (1.0 / (NB * NMP))
-    put_p.wait()
-    put_q.wait()
+    puts[3].start()
+    for put in puts:
+        put.wait()
 
 
 def run_finish(loss, hidden, total):
-    smem = pl.BlockSpec(memory_space=pltpu.SMEM)
     vmem = pl.BlockSpec(memory_space=pltpu.VMEM)
     hbm = pl.BlockSpec(memory_space=pl.ANY)
     return pl.pallas_call(
@@ -430,9 +457,9 @@
             jax.ShapeDtypeStruct((PR, HID), BF16),
             jax.ShapeDtypeStruct((HID, DIM), F32),
         ),
-        in_specs=[smem, vmem, vmem],
-        out_specs=(smem, hbm, hbm, vmem),
-        scratch_shapes=[pltpu.SemaphoreType.DMA((2,))],
+        in_specs=[hbm, vmem, vmem],
+        out_specs=(hbm, hbm, hbm, hbm),
+        scratch_shapes=[pltpu.VMEM((HID, DIM), F32), pltpu.SemaphoreType.DMA((4,))],
         compiler_params=pltpu.CompilerParams(vmem_limit_bytes=16 * 1024 * 1024),
     )(loss, hidden, total)
 

time: 60.6 us -> 60.1 us (level)
    pallas_call x1, Pallas kernels: 2.75 us -> 1.56 us  [run_finish(): pl.pallas_call(finish_kernel, out_shape=(jax.ShapeDtypeStruct((QN,), F32)...]
    pallas_call x1, Pallas kernels: 57 us -> 57.8 us  [run_step(): pl.pallas_call(step_kernel, out_shape=(jax.ShapeDtypeStruct((QN,), F32),...]
where the time goes in v5:
time: 60.1 us; the launch traced here: 60 us
  Pallas kernels  59.3 us (99%)
  between operations  0.64 us (1%)
    pallas_call x1, Pallas kernels, run_step(): pl.pallas_call(step_kernel, out_shape=(jax.ShapeDtypeStruct((QN,), F32),...  57.8 us
    pallas_call x1, Pallas kernels, run_finish(): pl.pallas_call(finish_kernel, out_shape=(jax.ShapeDtypeStruct((QN,), F32)...  1.56 us

profile of v5, /device:TPU:1, one launch (start us, length us, event | category | flops | bytes accessed | tf_op | source)
XLA Modules:
  0.0 60.0 jit_solution(10232015898198747941)
XLA Ops:
  0.6 57.8 %shard_map.93 = (f32[8]{0:T(128)S(1)}, bf16[1536,768]{1,0:T(8,128)(2,1)S(1)}, bf16[768,128]{1,0:T(8,128)(2,1)S(1)}) custom-call(s32[8]{0:T(128)} %qlen_any.1, s32[10]{0:T(128)} %plen_any.1, s32[8]{0:T(128)} %pos_any.1, bf16[256,768]{1,0:T(8,128)(2,1)} %qh_any.1, bf16[1280,768]{1,0:T(8,128)(2,1)} %ph_any.1, bf16[768,128]{1,0:T(8,128)(2,1)} %proj_any.1), custom_call_target="tpu_custom_call" | custom-call | tf_op jit(solution)/shard_map/pallas_call | solution.py:396
  58.4 1.6 %shard_map.94 = (f32[8]{0:T(128)}, bf16[256,768]{1,0:T(8,128)(2,1)}, bf16[1280,768]{1,0:T(8,128)(2,1)}, f32[768,128]{1,0:T(8,128)}) custom-call(f32[8]{0:T(128)S(1)} %get-tuple-element.7.loss, bf16[1536,768]{1,0:T(8,128)(2,1)S(1)} %get-tuple-element.8.hidden, bf16[768,128]{1,0:T(8,128)(2,1)S(1)} %get-tuple-element.9.total), custom_call_target="tpu_custom_call" | custom-call | tf_op jit(solution)/shard_map/pallas_call | solution.py:452

commit v6 on v5

--- a/solution.py
+++ b/solution.py
@@ -53,7 +53,7 @@
     loss_out, hidden_out_ref, total_out,
     qlen, plen, pos, both, proj, qbuf, qunit, qrad, paug, ptr, punit, prad, power, gsim,
     tops, tots, score, keeps, coef, member, lse_own, lse_in, tq_out, tq_in, qscaled,
-    ppre, pre_t, pgrad, ppart, src, a1, a2, a3, a4, b1, b2, b3, b4, c1, c2, c3, c4, gathered,
+    ppre, pre_t, pgrad, ppart, src, a1, a2, a3, b1, b2, b3, c1, c2, c3, gathered,
     in_sem, qs, qr, ls, lr, ts, tr, push, pull,
 ):
     bi = lax.axis_index("batch")
@@ -67,17 +67,24 @@
     y = yh * NYL + yl
     xz = bi - yh
 
-    def at_y(spot):
-        return (xz + lax.div(spot, NYL), lax.rem(spot, NYL) * NC + core)
-
-    def at_z(spot):
-        return (bi + (spot - z) * NYH, mi)
-
-    def at_x(spot):
-        return (bi + (spot - x) * (NYH * NZ), mi)
+    cores = turned(core, NC)
+
+    def at_y(spot, side):
+        return (xz + lax.div(spot, NYL), lax.rem(spot, NYL) * NC + side)
+
+    def at_z(spot, side):
+        return (bi + (spot - z) * NYH, mi + (side - core))
+
+    def at_x(spot, side):
+        return (bi + (spot - x) * (NYH * NZ), mi + (side - core))
+
+    def pairs(here, count, place):
+        return [
+            (spot * NC + side, place(spot, side))
+            for a, spot in turned(here, count) for c, side in cores if a or c]
 
     def line(here, count, place):
-        return [(spot, place(spot)) for a, spot in turned(here, count) if a]
+        return [(spot, place(spot, core)) for a, spot in turned(here, count) if a]
 
     def ring_peer(hop):
         there = bi + hop
@@ -111,11 +118,13 @@
         return len(places)
 
     greeted = greet([ring[hop] for hop in HOPS])
+    y_pairs = pairs(y, NYH * NYL, at_y)
+    z_pairs = pairs(z, NZ, at_z)
+    x_pairs = pairs(x, NX, at_x)
     y_line = line(y, NYH * NYL, at_y)
     z_line = line(z, NZ, at_z)
     x_line = line(x, NX, at_x)
-    partner = [(NC - 1 - core, (bi, mi + (NC - 1 - 2 * core)))]
-    greeted += greet([where for _, where in y_line + z_line + x_line + partner])
+    greeted += greet([where for _, where in y_pairs + z_pairs + x_pairs])
 
     for copy in small:
         copy.wait()
@@ -299,17 +308,17 @@
     def added(box):
         return jnp.sum(box[...].astype(F32), axis=0).astype(BF16)
 
-    along_y, along_z, along_x, across = (y_line, y), (z_line, z), (x_line, x), (partner, core)
+    along_y, along_z, along_x = (y_line, y), (z_line, z), (x_line, x)
     plan = (
-        ((a1, a2, a3, a4), (along_y, along_z, along_x, across)),
-        ((b1, b2, b3, b4), (along_z, along_y, along_x, across)),
-        ((c1, c2, c3, c4), (along_x, along_y, along_z, across)),
+        ((c1, c2, c3), ((x_pairs, x * NC + core), along_y, along_z)),
+        ((a1, a2, a3), ((y_pairs, y * NC + core), along_z, along_x)),
+        ((b1, b2, b3), ((z_pairs, z * NC + core), along_y, along_x)),
     )
     share = HID // 3
     def arrived(n, hop):
         boxes, route = plan[n]
         peers = route[hop][0]
-        bulk(5 * n + hop, peers, boxes[hop].at[pl.ds(0, len(peers))]).wait_recv()
+        bulk(4 * n + hop, peers, boxes[hop].at[pl.ds(0, len(peers))]).wait_recv()
 
     for n, (boxes, route) in enumerate(plan):
         peers, mine = route[0]
@@ -319,7 +328,7 @@
         for t in range(share // DIM):
             src[n * share + t * DIM:n * share + (t + 1) * DIM, :] = (
                 part[:, t * DIM:(t + 1) * DIM].astype(BF16))
-        start(5 * n, peers, lambda j: src.at[piece(n * share, size, j)], lambda j: boxes[0].at[j], mine)
+        start(4 * n, peers, lambda j: src.at[piece(n * share, size, j)], lambda j: boxes[0].at[j], mine)
         boxes[0][mine] = src[piece(n * share, size, mine), :]
 
     def hidden_tile(r):
@@ -333,51 +342,44 @@
         box = boxes[hop + 1]
         arrived(n, hop)
         box[here] = added(boxes[hop])
-        start(5 * n + hop + 1, peers, lambda j: box.at[here], lambda j: box.at[j], here)
+        start(4 * n + hop + 1, peers, lambda j: box.at[here], lambda j: box.at[j], here)
 
     def share_out(n):
         boxes, route = plan[n]
         peers, mine = route[0]
         size = boxes[0].shape[1]
-        arrived(n, 3)
-        gathered[piece(n * share, size, mine), :] = added(boxes[3])
+        arrived(n, 2)
+        gathered[piece(n * share, size, mine), :] = added(boxes[2])
         start(
-            5 * n + 4, peers, lambda j: gathered.at[piece(n * share, size, mine)],
+            4 * n + 3, peers, lambda j: gathered.at[piece(n * share, size, mine)],
             lambda j: gathered.at[piece(n * share, size, j)], mine)
 
     loss = total - jnp.sum(onehot * score[0], axis=0, keepdims=True)
     for q in range(QN):
         loss_out[q] = jnp.sum(jnp.where(lane == q * QT, loss, 0.0))
-    hidden_tile(0)
-    hidden_tile(1)
-    for n in range(3):
-        onward(n, 0)
-    hidden_tile(2)
-    hidden_tile(3)
-    for n in (2, 0, 1):
-        onward(n, 1)
+    for hop in range(2):
+        hidden_tile(2 * hop)
+        hidden_tile(2 * hop + 1)
+        for n in range(3):
+            onward(n, hop)
     hidden_tile(4)
     hidden_tile(5)
-    for n in (0, 1):
-        onward(n, 2)
-    for n in (0, 1):
+    for n in (1, 2, 0):
         share_out(n)
-    onward(2, 2)
-    share_out(2)
 
     def spread(n):
         boxes, route = plan[n]
         peers = route[0][0]
-        return bulk(5 * n + 4, peers, gathered.at[pl.ds(n * share, len(peers) * boxes[0].shape[1])])
+        return bulk(4 * n + 3, peers, gathered.at[pl.ds(n * share, len(peers) * boxes[0].shape[1])])
 
     for n in range(3):
         spread(n).wait_recv()
     total_out[...] = gathered[...]
 
     for n, (boxes, route) in enumerate(plan):
-        for hop in range(4):
+        for hop in range(3):
             peers = route[hop][0]
-            bulk(5 * n + hop, peers, boxes[hop].at[pl.ds(0, len(peers))]).wait_send()
+            bulk(4 * n + hop, peers, boxes[hop].at[pl.ds(0, len(peers))]).wait_send()
         spread(n).wait_send()
     for b in (1, 2):
         send_query(b).wait_send()
@@ -393,6 +395,7 @@
     vm = pltpu.VMEM
     ny = NYH * NYL
     share = HID // 3
+    ya, za, xa = ny * NC, NZ * NC, NX * NC
     return pl.pallas_call(
         step_kernel,
         out_shape=(
@@ -415,15 +418,12 @@
             vm((PR, DIM), BF16), vm((DIM, PR + QR), BF16),
             vm((PR, DIM), F32), vm((DIM, HID), F32),
             vm((HID, DIM), BF16),
-            vm((ny, share // ny, DIM), BF16), vm((NZ, share // ny, DIM), BF16),
-            vm((NX, share // ny, DIM), BF16), vm((NC, share // ny, DIM), BF16),
-            vm((NZ, share // NZ, DIM), BF16), vm((ny, share // NZ, DIM), BF16),
-            vm((NX, share // NZ, DIM), BF16), vm((NC, share // NZ, DIM), BF16),
-            vm((NX, share // NX, DIM), BF16), vm((ny, share // NX, DIM), BF16),
-            vm((NZ, share // NX, DIM), BF16), vm((NC, share // NX, DIM), BF16),
+            vm((ya, share // ya, DIM), BF16), vm((NZ, share // ya, DIM), BF16), vm((NX, share // ya, DIM), BF16),
+            vm((za, share // za, DIM), BF16), vm((ny, share // za, DIM), BF16), vm((NX, share // za, DIM), BF16),
+            vm((xa, share // xa, DIM), BF16), vm((ny, share // xa, DIM), BF16), vm((NZ, share // xa, DIM), BF16),
             vm((HID, DIM), BF16),
             dma((6,)), dma((2,)), dma((2,)), dma((4,)), dma((4,)), dma((2,)), dma((2,)),
-            dma((15,)), dma((15,)),
+            dma((12,)), dma((12,)),
         ],
         compiler_params=pltpu.CompilerParams(
             collective_id=0, has_side_effects=True, vmem_limit_bytes=24 * 1024 * 1024),

time: 60.1 us -> 58 us (0.965)
  Pallas kernels: 59.3 us -> 57.3 us
    pallas_call x1, Pallas kernels: 57.8 us -> 55.7 us  [run_step(): pl.pallas_call(step_kernel, out_shape=(jax.ShapeDtypeStruct((QN,), F32),...]
where the time goes in v6:
time: 58 us; the launch traced here: 57.9 us
  Pallas kernels  57.3 us (99%)
  between operations  0.64 us (1%)
    pallas_call x1, Pallas kernels, run_step(): pl.pallas_call(step_kernel, out_shape=(jax.ShapeDtypeStruct((QN,), F32),...  55.7 us
    pallas_call x1, Pallas kernels, run_finish(): pl.pallas_call(finish_kernel, out_shape=(jax.ShapeDtypeStruct((QN,), F32)...  1.56 us

profile of v6, /device:TPU:1, one launch (start us, length us, event | category | flops | bytes accessed | tf_op | source)
XLA Modules:
  0.0 57.9 jit_solution(3557047352705819081)
XLA Ops:
  0.6 55.7 %shard_map.93 = (f32[8]{0:T(128)S(1)}, bf16[1536,768]{1,0:T(8,128)(2,1)S(1)}, bf16[768,128]{1,0:T(8,128)(2,1)S(1)}) custom-call(s32[8]{0:T(128)} %qlen_any.1, s32[10]{0:T(128)} %plen_any.1, s32[8]{0:T(128)} %pos_any.1, bf16[256,768]{1,0:T(8,128)(2,1)} %qh_any.1, bf16[1280,768]{1,0:T(8,128)(2,1)} %ph_any.1, bf16[768,128]{1,0:T(8,128)(2,1)} %proj_any.1), custom_call_target="tpu_custom_call" | custom-call | tf_op jit(solution)/shard_map/pallas_call | solution.py:399
  56.3 1.6 %shard_map.94 = (f32[8]{0:T(128)}, bf16[256,768]{1,0:T(8,128)(2,1)}, bf16[1280,768]{1,0:T(8,128)(2,1)}, f32[768,128]{1,0:T(8,128)}) custom-call(f32[8]{0:T(128)S(1)} %get-tuple-element.7.loss, bf16[1536,768]{1,0:T(8,128)(2,1)S(1)} %get-tuple-element.8.hidden, bf16[768,128]{1,0:T(8,128)(2,1)S(1)} %get-tuple-element.9.total), custom_call_target="tpu_custom_call" | custom-call | tf_op jit(solution)/shard_map/pallas_call | solution.py:452

commit v7 on v6

--- a/solution.py
+++ b/solution.py
@@ -118,13 +118,10 @@
         return len(places)
 
     greeted = greet([ring[hop] for hop in HOPS])
-    y_pairs = pairs(y, NYH * NYL, at_y)
-    z_pairs = pairs(z, NZ, at_z)
     x_pairs = pairs(x, NX, at_x)
     y_line = line(y, NYH * NYL, at_y)
     z_line = line(z, NZ, at_z)
-    x_line = line(x, NX, at_x)
-    greeted += greet([where for _, where in y_pairs + z_pairs + x_pairs])
+    greeted += greet([where for _, where in y_line + z_line + x_pairs])
 
     for copy in small:
         copy.wait()
@@ -308,11 +305,11 @@
     def added(box):
         return jnp.sum(box[...].astype(F32), axis=0).astype(BF16)
 
-    along_y, along_z, along_x = (y_line, y), (z_line, z), (x_line, x)
+    along_y, along_z, around_x = (y_line, y), (z_line, z), (x_pairs, x * NC + core)
     plan = (
-        ((c1, c2, c3), ((x_pairs, x * NC + core), along_y, along_z)),
-        ((a1, a2, a3), ((y_pairs, y * NC + core), along_z, along_x)),
-        ((b1, b2, b3), ((z_pairs, z * NC + core), along_y, along_x)),
+        ((c1, c2, c3), (around_x, along_y, along_z)),
+        ((a1, a2, a3), (along_y, along_z, around_x)),
+        ((b1, b2, b3), (along_z, along_y, around_x)),
     )
     share = HID // 3
     def arrived(n, hop):
@@ -395,7 +392,7 @@
     vm = pltpu.VMEM
     ny = NYH * NYL
     share = HID // 3
-    ya, za, xa = ny * NC, NZ * NC, NX * NC
+    xa = NX * NC
     return pl.pallas_call(
         step_kernel,
         out_shape=(
@@ -418,8 +415,8 @@
             vm((PR, DIM), BF16), vm((DIM, PR + QR), BF16),
             vm((PR, DIM), F32), vm((DIM, HID), F32),
             vm((HID, DIM), BF16),
-            vm((ya, share // ya, DIM), BF16), vm((NZ, share // ya, DIM), BF16), vm((NX, share // ya, DIM), BF16),
-            vm((za, share // za, DIM), BF16), vm((ny, share // za, DIM), BF16), vm((NX, share // za, DIM), BF16),
+            vm((ny, share // ny, DIM), BF16), vm((NZ, share // ny, DIM), BF16), vm((xa, share // ny, DIM), BF16),
+            vm((NZ, share // NZ, DIM), BF16), vm((ny, share // NZ, DIM), BF16), vm((xa, share // NZ, DIM), BF16),
             vm((xa, share // xa, DIM), BF16), vm((ny, share // xa, DIM), BF16), vm((NZ, share // xa, DIM), BF16),
             vm((HID, DIM), BF16),
             dma((6,)), dma((2,)), dma((2,)), dma((4,)), dma((4,)), dma((2,)), dma((2,)),

time: 58 us -> 58 us (level)
  no operation moved by 1% of the time
where the time goes in v7:
time: 58 us; the launch traced here: 57.9 us
  Pallas kernels  57.2 us (99%)
  between operations  0.64 us (1%)
    pallas_call x1, Pallas kernels, run_step(): pl.pallas_call(step_kernel, out_shape=(jax.ShapeDtypeStruct((QN,), F32),...  55.7 us
    pallas_call x1, Pallas kernels, run_finish(): pl.pallas_call(finish_kernel, out_shape=(jax.ShapeDtypeStruct((QN,), F32)...  1.56 us

profile of v7, /device:TPU:1, one launch (start us, length us, event | category | flops | bytes accessed | tf_op | source)
XLA Modules:
  0.0 57.9 jit_solution(18372108421055149381)
XLA Ops:
  0.6 55.7 %shard_map.93 = (f32[8]{0:T(128)S(1)}, bf16[1536,768]{1,0:T(8,128)(2,1)S(1)}, bf16[768,128]{1,0:T(8,128)(2,1)S(1)}) custom-call(s32[8]{0:T(128)} %qlen_any.1, s32[10]{0:T(128)} %plen_any.1, s32[8]{0:T(128)} %pos_any.1, bf16[256,768]{1,0:T(8,128)(2,1)} %qh_any.1, bf16[1280,768]{1,0:T(8,128)(2,1)} %ph_any.1, bf16[768,128]{1,0:T(8,128)(2,1)} %proj_any.1), custom_call_target="tpu_custom_call" | custom-call | tf_op jit(solution)/shard_map/pallas_call | solution.py:396
  56.3 1.6 %shard_map.94 = (f32[8]{0:T(128)}, bf16[256,768]{1,0:T(8,128)(2,1)}, bf16[1280,768]{1,0:T(8,128)(2,1)}, f32[768,128]{1,0:T(8,128)}) custom-call(f32[8]{0:T(128)S(1)} %get-tuple-element.7.loss, bf16[1536,768]{1,0:T(8,128)(2,1)S(1)} %get-tuple-element.8.hidden, bf16[768,128]{1,0:T(8,128)(2,1)S(1)} %get-tuple-element.9.total), custom_call_target="tpu_custom_call" | custom-call | tf_op jit(solution)/shard_map/pallas_call | solution.py:449

commit v8 on v7

--- a/solution.py
+++ b/solution.py
@@ -23,6 +23,7 @@
 HOPS = (1, 2, -1, -2)
 LSE_READY = (1, 0, 2, 2)
 CHUNK = 256
+ROWS = 256
 UNROLL = 2
 
 
@@ -170,8 +171,8 @@
 
     get_ph.wait()
 
-    for r in range(PR // CHUNK):
-        spot = pl.ds(r * CHUNK, CHUNK)
+    for r in range(PR // ROWS):
+        spot = pl.ds(r * ROWS, ROWS)
         before = jnp.dot(both[spot, :], proj[...], preferred_element_type=F32)
         radius = jnp.sqrt(jnp.sum(before * before, axis=-1, keepdims=True) + norm_eps)
         inverse = 1.0 / radius
@@ -180,7 +181,7 @@
         prad[spot, :] = inverse
         embed = unit.astype(BF16)
         paug[spot, :DIM] = embed * jnp.array(inner_scale, BF16)
-        ptr[:, spot] = embed.astype(F32).T.astype(BF16)
+        ptr[:, spot] = embed.T
 
     def forward(b):
         power[b] = jnp.dot(paug[...], qbuf[b], preferred_element_type=F32)
@@ -267,14 +268,14 @@
     total = log_sum((lse_own[2, 0:1, :], lse_in[2, 1:2, :], lse_in[3, 2:3, :]))
     to_grads(0, jnp.exp(score[0] - total) - onehot)
 
-    for r in range(PR // CHUNK):
-        spot = pl.ds(r * CHUNK, CHUNK)
+    for r in range(PR // ROWS):
+        spot = pl.ds(r * ROWS, ROWS)
         grad = pgrad[spot, :] + nt_dot(gsim[0, spot, :], qbuf[0, :DIM, :])
         unit = punit[spot, :]
         pre = (grad - unit * jnp.sum(unit * grad, axis=-1, keepdims=True)) * prad[spot, :]
         pre = pre.astype(BF16)
         ppre[spot, :] = pre
-        pre_t[:, spot] = pre.astype(F32).T.astype(BF16)
+        pre_t[:, spot] = pre.T
 
     ppart[...] = jnp.dot(pre_t[:, whole_p], both[whole_p, :], preferred_element_type=F32)
     qgrad = jnp.dot(ptr[...], gsim[0], preferred_element_type=F32)
@@ -307,9 +308,9 @@
 
     along_y, along_z, around_x = (y_line, y), (z_line, z), (x_pairs, x * NC + core)
     plan = (
-        ((c1, c2, c3), (around_x, along_y, along_z)),
         ((a1, a2, a3), (along_y, along_z, around_x)),
         ((b1, b2, b3), (along_z, along_y, around_x)),
+        ((c1, c2, c3), (around_x, along_y, along_z)),
     )
     share = HID // 3
     def arrived(n, hop):
@@ -357,11 +358,11 @@
     for hop in range(2):
         hidden_tile(2 * hop)
         hidden_tile(2 * hop + 1)
-        for n in range(3):
+        for n in (2, 0, 1):
             onward(n, hop)
     hidden_tile(4)
     hidden_tile(5)
-    for n in (1, 2, 0):
+    for n in (0, 1, 2):
         share_out(n)
 
     def spread(n):

time: 58 us -> 57.6 us (level)
  no operation moved by 1% of the time
where the time goes in v8:
time: 57.6 us; the launch traced here: 57.5 us
  Pallas kernels  56.8 us (99%)
  between operations  0.64 us (1%)
    pallas_call x1, Pallas kernels, run_step(): pl.pallas_call(step_kernel, out_shape=(jax.ShapeDtypeStruct((QN,), F32),...  55.3 us
    pallas_call x1, Pallas kernels, run_finish(): pl.pallas_call(finish_kernel, out_shape=(jax.ShapeDtypeStruct((QN,), F32)...  1.56 us

profile of v8, /device:TPU:1, one launch (start us, length us, event | category | flops | bytes accessed | tf_op | source)
XLA Modules:
  0.0 57.5 jit_solution(10700789629004332947)
XLA Ops:
  0.6 55.3 %shard_map.93 = (f32[8]{0:T(128)S(1)}, bf16[1536,768]{1,0:T(8,128)(2,1)S(1)}, bf16[768,128]{1,0:T(8,128)(2,1)S(1)}) custom-call(s32[8]{0:T(128)} %qlen_any.1, s32[10]{0:T(128)} %plen_any.1, s32[8]{0:T(128)} %pos_any.1, bf16[256,768]{1,0:T(8,128)(2,1)} %qh_any.1, bf16[1280,768]{1,0:T(8,128)(2,1)} %ph_any.1, bf16[768,128]{1,0:T(8,128)(2,1)} %proj_any.1), custom_call_target="tpu_custom_call" | custom-call | tf_op jit(solution)/shard_map/pallas_call | solution.py:397
  55.9 1.6 %shard_map.94 = (f32[8]{0:T(128)}, bf16[256,768]{1,0:T(8,128)(2,1)}, bf16[1280,768]{1,0:T(8,128)(2,1)}, f32[768,128]{1,0:T(8,128)}) custom-call(f32[8]{0:T(128)S(1)} %get-tuple-element.7.loss, bf16[1536,768]{1,0:T(8,128)(2,1)S(1)} %get-tuple-element.8.hidden, bf16[768,128]{1,0:T(8,128)(2,1)S(1)} %get-tuple-element.9.total), custom_call_target="tpu_custom_call" | custom-call | tf_op jit(solution)/shard_map/pallas_call | solution.py:450
